TPU v7x, 256 devices: a whole 4x4x8 slice. The times are simulated.
256 devices in a mesh: frames: 32 (over z, x_hi, core), heads: 8 (over y, x_lo).
Axes of the slice: x: 4 (x_hi: 2, x_lo: 2; x = x_hi * 2 + x_lo), y: 4, z: 8, core: 2. Of those that a mesh axis runs over, the one named last changes fastest.
Arguments:
- queries: bfloat16 [32768, 3072], P(('frames', 'heads')), may hold values from -6 to 6
- key_rows: bfloat16 [32768, 3072], P(('frames', 'heads')), may hold values from -6 to 6
- value_rows: bfloat16 [32768, 3072], P(('frames', 'heads')), may hold values from -6 to 6
- out_grad: bfloat16 [32768, 3072], P(('frames', 'heads')), may hold values from -6 to 6
- key_tiles: int32 [128, 8], P('frames'), may hold values from 0 to 127, as said below
- key_count: int32 [128], P('frames'), may hold values from 2 to 8, as said below
Outputs:
- attended: bfloat16 [32768, 3072], P(('frames', 'heads'))
- query_grad: bfloat16 [32768, 3072], P(('frames', 'heads'))
- key_grad: bfloat16 [32768, 3072], P(('frames', 'heads'))
- value_grad: bfloat16 [32768, 3072], P(('frames', 'heads'))
Inputs may be any that keep to these rules, and one draw needn't show every extreme that they name: `key_tiles`: the first entry of each row is the row's own tile; a row may list the same tile id more than once; every id lies in the row's aligned group of 4 consecutive tiles or in one of the two neighbouring groups; entries at or after key_count are the row's own tile. `key_count`: some tile of every aligned group of 4 tiles uses all 8 entries.
All inputs are finite; a program needn't handle non-finite values.
Results may differ from a plain program's by a relative error of at most 0.022.
Values may be sent and summed in bfloat16 or wider, within the bound.
A program may use at most 128 MiB of HBM per device.

v0:
```python
import jax
import jax.numpy as jnp
from jax import lax
from jax.sharding import PartitionSpec as P

HEAD_DIM = 128
TILE = 256


def extended(cells, sides, width):
    for axis, dim in sides:
        count = lax.axis_size(axis)
        ends = count - 1
        head = lax.slice_in_dim(cells, 0, width, axis=dim)
        tail = lax.slice_in_dim(cells, cells.shape[dim] - width, cells.shape[dim], axis=dim)
        cells = jnp.concatenate(
            [
                lax.ppermute(tail, axis, [(i, (i + 1) % count) for i in range(ends)]),
                cells,
                lax.ppermute(head, axis, [((i + 1) % count, i) for i in range(ends)]),
            ],
            axis=dim,
        )
    return cells


def shifted(array, axis, by):
    length = lax.axis_size(axis)
    pairs = [(i, i + by) for i in range(length) if 0 <= i + by < length]
    return lax.ppermute(array, axis, pairs)


def tile_forward(query_tile, grad_tile, key_sel, value_sel, allowed, score_scale):
    scores = (
        jnp.einsum("qhd,khd->hqk", query_tile, key_sel, preferred_element_type=jnp.float32)
        * score_scale
    )
    scores = jnp.where(allowed[None, None, :], scores, -jnp.inf)
    highest = jnp.max(scores, axis=-1)
    log_total = highest + jnp.log(jnp.sum(jnp.exp(scores - highest[..., None]), axis=-1))
    weights = jnp.exp(scores - log_total[..., None])
    weights_low = weights.astype(jnp.bfloat16)
    attended = jnp.einsum(
        "hqk,khd->qhd", weights_low, value_sel, preferred_element_type=jnp.float32
    ).astype(jnp.bfloat16)
    row_dots = jnp.einsum("qhd,qhd->hq", grad_tile, attended, preferred_element_type=jnp.float32)
    d_weights = jnp.einsum("qhd,khd->hqk", grad_tile, value_sel, preferred_element_type=jnp.float32)
    d_scores = (weights * (d_weights - row_dots[..., None])).astype(jnp.bfloat16)
    query_grad = (
        jnp.einsum("hqk,khd->qhd", d_scores, key_sel, preferred_element_type=jnp.float32)
        * score_scale
    ).astype(jnp.bfloat16)
    return (attended, log_total, row_dots, query_grad, weights_low, d_scores)


def key_side(query_tile, grad_tile, weights_low, d_scores, score_scale):
    key_part = (
        jnp.einsum("hqk,qhd->khd", d_scores, query_tile, preferred_element_type=jnp.float32)
        * score_scale
    )
    value_part = jnp.einsum(
        "hqk,qhd->khd", weights_low, grad_tile, preferred_element_type=jnp.float32
    )
    key_rows_count = key_part.shape[0]
    return jnp.concatenate(
        [key_part.reshape(key_rows_count, -1), value_part.reshape(key_rows_count, -1)], axis=1
    )


def on_device(queries, key_rows, value_rows, out_grad, key_tiles, key_count):
    own_query, own_key, own_value, own_grad = (
        lax.all_to_all(queries, "heads", split_axis=1, concat_axis=0, tiled=True),
        lax.all_to_all(key_rows, "heads", split_axis=1, concat_axis=0, tiled=True),
        lax.all_to_all(value_rows, "heads", split_axis=1, concat_axis=0, tiled=True),
        lax.all_to_all(out_grad, "heads", split_axis=1, concat_axis=0, tiled=True),
    )
    slab_rows, features = own_query.shape
    tiles_dev, entries = key_tiles.shape
    heads_dev = features // HEAD_DIM
    score_scale = HEAD_DIM ** (-0.5)
    kv_own = jnp.concatenate([own_key, own_value], axis=1)
    kv_buffer = extended(kv_own, (("frames", 0),), slab_rows)
    first_tile = (lax.axis_index("frames") - 1) * tiles_dev
    query_tiles = own_query.reshape(tiles_dev, TILE, heads_dev, HEAD_DIM)
    grad_tiles = own_grad.reshape(tiles_dev, TILE, heads_dev, HEAD_DIM)

    def per_tile(totals, inputs):
        query_tile, grad_tile, tile_ids, tile_count = inputs
        local_tiles = tile_ids - first_tile
        blocks = [
            lax.dynamic_slice_in_dim(kv_buffer, local_tiles[entry_pos] * TILE, TILE, 0)
            for entry_pos in range(entries)
        ]
        picked = jnp.concatenate(blocks, axis=0)
        key_sel = picked[:, :features].reshape(-1, heads_dev, HEAD_DIM)
        value_sel = picked[:, features:].reshape(-1, heads_dev, HEAD_DIM)
        allowed = jnp.repeat(jnp.arange(entries, dtype=jnp.int32) < tile_count, TILE)
        attended, log_total, row_dots, query_grad, weights_low, d_scores = tile_forward(
            query_tile, grad_tile, key_sel, value_sel, allowed, score_scale
        )
        grad_part = key_side(query_tile, grad_tile, weights_low, d_scores, score_scale)
        for entry_pos in range(entries):
            block_start = local_tiles[entry_pos] * TILE
            current = lax.dynamic_slice_in_dim(totals, block_start, TILE, 0)
            totals = lax.dynamic_update_slice_in_dim(
                totals,
                current + grad_part[entry_pos * TILE : (entry_pos + 1) * TILE],
                block_start,
                0,
            )
        return (
            totals,
            (
                attended.reshape(TILE, features),
                query_grad.reshape(TILE, features),
                log_total,
                row_dots,
            ),
        )

    start_totals = jnp.zeros((3 * slab_rows, 2 * features), jnp.float32)
    totals, (attended, query_grad, log_total, row_dots) = lax.scan(
        per_tile, start_totals, (query_tiles, grad_tiles, key_tiles, key_count)
    )
    attended = attended.reshape(slab_rows, features)
    query_grad = query_grad.reshape(slab_rows, features)
    from_above = shifted(totals[:slab_rows], "frames", -1)
    from_below = shifted(totals[2 * slab_rows :], "frames", 1)
    kv_grad = totals[slab_rows : 2 * slab_rows] + from_above + from_below
    key_grad = kv_grad[:, :features].astype(jnp.bfloat16)
    value_grad = kv_grad[:, features:].astype(jnp.bfloat16)
    return (
        lax.all_to_all(attended, "heads", split_axis=0, concat_axis=1, tiled=True),
        lax.all_to_all(query_grad, "heads", split_axis=0, concat_axis=1, tiled=True),
        lax.all_to_all(key_grad, "heads", split_axis=0, concat_axis=1, tiled=True),
        lax.all_to_all(value_grad, "heads", split_axis=0, concat_axis=1, tiled=True),
    )


def solution(mesh):
    placed = (
        P(("frames", "heads"), None),
        P(("frames", "heads"), None),
        P(("frames", "heads"), None),
        P(("frames", "heads"), None),
        P("frames", None),
        P("frames"),
    )
    return jax.shard_map(
        on_device,
        mesh=mesh,
        in_specs=placed,
        out_specs=(
            P(("frames", "heads"), None),
            P(("frames", "heads"), None),
            P(("frames", "heads"), None),
            P(("frames", "heads"), None),
        ),
        check_vma=False,
    )
```

profile of v0, /device:TPU:100, one launch (start us, length us, event | category | flops | bytes accessed | tf_op | source)
XLA Modules:
  0.0 489.1 jit_solution(1486168622863203848)
XLA Ops:
  0.6 2.3 copy.76
  2.9 5.1 %all-to-all-start.1 = ((bf16[128,8,384]{0,2,1:T(8,128)(2,1)}), bf16[128,8,384]{0,2,1:T(8,128)(2,1)S(1)}, u32[]{:S(2)}, u32[]{:S(2)}) async-start(bf16[128,8,384]{0,2,1:T(8,128)(2,1)} %bitcast.27), calls=%async_computation.1 | async-start | bytes 1572864 | tf_op jit(solution)/shard_map/all_to_all | solution.py:73
  8.0 2.4 copy.78
  10.4 10.5 %all-to-all-done.1 = bf16[128,8,384]{0,2,1:T(8,128)(2,1)S(1)} async-done(((bf16[128,8,384]{0,2,1:T(8,128)(2,1)}), bf16[128,8,384]{0,2,1:T(8,128)(2,1)S(1)}, u32[]{:S(2)}, u32[]{:S(2)}) %all-to-all-start.1) | async-done | bytes 786464 | tf_op jit(solution)/shard_map/all_to_all | solution.py:73
  20.9 3.5 all-to-all-start.2
  24.8 11.7 %all-to-all-done.2 = bf16[128,8,384]{0,2,1:T(8,128)(2,1)S(1)} async-done(((bf16[128,8,384]{0,2,1:T(8,128)(2,1)}), bf16[128,8,384]{0,2,1:T(8,128)(2,1)S(1)}, u32[]{:S(2)}, u32[]{:S(2)}) %all-to-all-start.2) | async-done | bytes 786464 | tf_op jit(solution)/shard_map/all_to_all | solution.py:74
  40.1 2.4 collective-permute-start
  43.7 3.5 all-to-all-start
  47.2 2.3 copy.80
  49.5 40.1 %all-to-all-done = bf16[128,8,384]{0,2,1:T(8,128)(2,1)S(1)} async-done(((bf16[128,8,384]{0,2,1:T(8,128)(2,1)}), bf16[128,8,384]{0,2,1:T(8,128)(2,1)S(1)}, u32[]{:S(2)}, u32[]{:S(2)}) %all-to-all-start) | async-done | bytes 786464 | tf_op jit(solution)/shard_map/all_to_all | solution.py:72
  89.6 3.5 all-to-all-start.3
  98.0 5.2 %all-to-all-done.3 = bf16[128,8,384]{0,2,1:T(8,128)(2,1)S(1)} async-done(((bf16[128,8,384]{0,2,1:T(8,128)(2,1)}), bf16[128,8,384]{0,2,1:T(8,128)(2,1)S(1)}, u32[]{:S(2)}, u32[]{:S(2)}) %all-to-all-start.3) | async-done | bytes 786464 | tf_op jit(solution)/shard_map/all_to_all | solution.py:75
  105.7 5.0 %pad_maximum_fusion.1 = bf16[3072,768]{1,0:T(8,128)(2,1)} fusion(bf16[1024,768]{1,0:T(8,128)(2,1)} %collective-permute-done.1, bf16[1024,384]{1,0:T(8,128)(2,1)S(1)} %bitcast.157, bf16[1024,384]{1,0:T(8,128)(2,1)S(1)} %bitcast.155, bf16[1024,768]{1,0:T(8,128)(2,1)} %collective-permute-done), kind=kLoop, calls=%fused_computation.82 | loop fusion | flops 18874368 | bytes 9437184 | tf_op jit(solution)/shard_map/concatenate | solution.py:16
  110.8 6.7 %copy.83 = bf16[3072,768]{0,1:T(8,128)(2,1)} copy(bf16[3072,768]{1,0:T(8,128)(2,1)} %pad_maximum_fusion.1) | data formatting | bytes 9437184 | tf_op jit(solution)/shard_map/while | solution.py:122
  117.4 4.8 broadcast_in_dim.30
  122.3 224.1 %while.14 = (s32[]{:T(128)}, f32[3072,768]{0,1:T(8,128)}, bf16[4,256,384]{2,1,0:T(8,128)(2,1)}, bf16[4,256,384]{2,1,0:T(8,128)(2,1)}, s32[4,8]{1,0:T(4,128)}, /*...) while((s32[]{:T(128)}, f32[3072,768]{0,1:T(8,128)}, ...), condition=%wide.region_3.4_spmd, body=%wide.region_0.3_spmd.sunk | while | flops 2453568000 | bytes 209045408 | solution.py:122
  139.7 2.3 fusion.94
  145.2 5.4 %multiply_convert_fusion.2 = bf16[3,256,2048]{2,1,0:T(8,128)(2,1)S(1)} fusion(f32[3,256,2048]{2,1,0:T(8,128)} %copy-done.1, bf16[2048,3,128]{0,2,1:T(8,128)(2,1)} %bitcast.152, f32[3,256]{1,0:T(4,128)S(1)} %get-tuple-element.242, f32[3,256]{1,0:T(4,128)S(1)} %log_add_fusion.2, pred[2048]{0:T(1024)(128)(4,1)S(1)} %broadcast_in_dim.70, ...), kind=kOutput, calls=%fused_computation.14.clone.1 | convolution fusion | flops 412090368 | bytes 11214852 | tf_op jit(solution)/shard_map/while/body/eval_jaxpr/qhd,khd->hqk/dot_general | solution.py:47
  150.6 4.2 fusion.95
  160.4 2.3 fusion.96
  162.7 2.2 fusion.97
  167.1 2.2 fusion.99
  169.3 2.2 fusion.100
  171.6 2.2 fusion.101
  173.8 2.3 fusion.102
  176.1 2.2 fusion.103
  195.8 2.3 fusion.94
  201.2 5.4 %multiply_convert_fusion.2 = bf16[3,256,2048]{2,1,0:T(8,128)(2,1)S(1)} fusion(f32[3,256,2048]{2,1,0:T(8,128)} %copy-done.1, bf16[2048,3,128]{0,2,1:T(8,128)(2,1)} %bitcast.152, f32[3,256]{1,0:T(4,128)S(1)} %get-tuple-element.242, f32[3,256]{1,0:T(4,128)S(1)} %log_add_fusion.2, pred[2048]{0:T(1024)(128)(4,1)S(1)} %broadcast_in_dim.70, ...), kind=kOutput, calls=%fused_computation.14.clone.1 | convolution fusion | flops 412090368 | bytes 11214852 | tf_op jit(solution)/shard_map/while/body/eval_jaxpr/qhd,khd->hqk/dot_general | solution.py:47
  206.7 4.2 fusion.95
  216.4 2.3 fusion.96
  218.8 2.2 fusion.97
  223.2 2.3 fusion.99
  225.4 2.2 fusion.100
  229.9 2.2 fusion.102
  232.1 2.2 fusion.103
  251.8 2.3 fusion.94
  257.2 5.4 %multiply_convert_fusion.2 = bf16[3,256,2048]{2,1,0:T(8,128)(2,1)S(1)} fusion(f32[3,256,2048]{2,1,0:T(8,128)} %copy-done.1, bf16[2048,3,128]{0,2,1:T(8,128)(2,1)} %bitcast.152, f32[3,256]{1,0:T(4,128)S(1)} %get-tuple-element.242, f32[3,256]{1,0:T(4,128)S(1)} %log_add_fusion.2, pred[2048]{0:T(1024)(128)(4,1)S(1)} %broadcast_in_dim.70, ...), kind=kOutput, calls=%fused_computation.14.clone.1 | convolution fusion | flops 412090368 | bytes 11214852 | tf_op jit(solution)/shard_map/while/body/eval_jaxpr/qhd,khd->hqk/dot_general | solution.py:47
  262.7 4.2 fusion.95
  272.4 2.3 fusion.96
  274.8 2.2 fusion.97
  279.2 2.2 fusion.99
  288.1 2.2 fusion.103
  307.7 2.3 fusion.94
  313.2 5.4 %multiply_convert_fusion.2 = bf16[3,256,2048]{2,1,0:T(8,128)(2,1)S(1)} fusion(f32[3,256,2048]{2,1,0:T(8,128)} %copy-done.1, bf16[2048,3,128]{0,2,1:T(8,128)(2,1)} %bitcast.152, f32[3,256]{1,0:T(4,128)S(1)} %get-tuple-element.242, f32[3,256]{1,0:T(4,128)S(1)} %log_add_fusion.2, pred[2048]{0:T(1024)(128)(4,1)S(1)} %broadcast_in_dim.70, ...), kind=kOutput, calls=%fused_computation.14.clone.1 | convolution fusion | flops 412090368 | bytes 11214852 | tf_op jit(solution)/shard_map/while/body/eval_jaxpr/qhd,khd->hqk/dot_general | solution.py:47
  318.6 4.2 fusion.95
  328.4 2.3 fusion.96
  330.7 2.2 fusion.97
  333.0 2.2 fusion.98
  335.2 2.2 fusion.99
  337.5 2.2 fusion.100
  339.7 2.2 fusion.101
  341.9 2.2 fusion.102
  344.2 2.2 fusion.103
  346.4 6.7 %fusion.49 = (f32[1024,768]{0,1:T(8,128)}, f32[1024,768]{0,1:T(8,128)}) fusion(f32[3072,768]{0,1:T(8,128)} %get-tuple-element.60), kind=kLoop, calls=%fused_computation.87 | loop fusion | bytes 12582912 | tf_op jit(solution)/shard_map/slice | solution.py:127
  353.1 3.8 collective-permute-start.2
  358.8 85.9 %all_to_all.146 = bf16[8,128,384]{2,1,0:T(8,128)(2,1)S(1)} all-to-all(bf16[8,128,384]{2,1,0:T(8,128)(2,1)S(1)} %bitcast.167), channel_id=1, replica_groups=mesh['frames'=32,'heads'=8] {'heads'}, dimensions={0} | all-to-all | bytes 1572864 | tf_op jit(solution)/shard_map/all_to_all | solution.py:133
  444.6 5.5 %all-to-all-start.5 = ((bf16[8,128,384]{2,1,0:T(8,128)(2,1)}), bf16[8,128,384]{2,1,0:T(8,128)(2,1)S(1)}, u32[]{:S(2)}, u32[]{:S(2)}) async-start(bf16[8,128,384]{2,1,0:T(8,128)(2,1)} %bitcast.38), calls=%async_computation.5 | async-start | bytes 1572864 | tf_op jit(solution)/shard_map/all_to_all | solution.py:134
  450.2 4.6 add_convert_fusion
  456.1 4.2 all-to-all-done.5
  460.3 3.5 all-to-all-start.7
  465.0 8.9 %all-to-all-done.7 = bf16[8,128,384]{2,1,0:T(8,128)(2,1)S(1)} async-done(((bf16[8,128,384]{2,1,0:T(8,128)(2,1)}), bf16[8,128,384]{2,1,0:T(8,128)(2,1)S(1)}, u32[]{:S(2)}, u32[]{:S(2)}) %all-to-all-start.7) | async-done | bytes 786464 | tf_op jit(solution)/shard_map/all_to_all | solution.py:136
  473.9 3.5 all-to-all-start.6
  478.6 2.3 copy.93
  484.0 3.5 all-to-all-done.6
  (201 shorter events, 121.9 us)
Async XLA Ops:
  2.9 18.0 %all-to-all-start.1 = ((bf16[128,8,384]{0,2,1:T(8,128)(2,1)}), bf16[128,8,384]{0,2,1:T(8,128)(2,1)S(1)}, u32[]{:S(2)}, u32[]{:S(2)}) async-start(bf16[128,8,384]{0,2,1:T(8,128)(2,1)} %bitcast.27), calls=%async_computation.1 | async-start | bytes 1572864 | tf_op jit(solution)/shard_map/all_to_all | solution.py:73
  8.0 34.5 %copy-start.5 = (bf16[128,3072]{1,0:T(8,128)(2,1)S(1)}, bf16[128,3072]{1,0:T(8,128)(2,1)}, u32[]{:S(2)}) copy-start(bf16[128,3072]{1,0:T(8,128)(2,1)} %param.8) | copy-start | bytes 2359300
  20.9 15.6 %all-to-all-start.2 = ((bf16[128,8,384]{0,2,1:T(8,128)(2,1)}), bf16[128,8,384]{0,2,1:T(8,128)(2,1)S(1)}, u32[]{:S(2)}, u32[]{:S(2)}) async-start(bf16[128,8,384]{0,2,1:T(8,128)(2,1)} %bitcast.30), calls=%async_computation.2 | async-start | bytes 1572864 | tf_op jit(solution)/shard_map/all_to_all | solution.py:74
  38.2 67.5 %collective-permute-start.1 = (bf16[1024,768]{1,0:T(8,128)(2,1)}, bf16[1024,768]{1,0:T(8,128)(2,1)}, u32[]{:S(2)}, u32[]{:S(2)}) collective-permute-start(bf16[1024,768]{1,0:T(8,128)(2,1)} %pad_maximum_fusion.2), channel_id=1, source_target_pairs={{8,0},{16,8},{24,16},{32,24},{40,32},{48,40},{56,48},{64,56},{72,6... | collective-permute-start | bytes 4718600 | tf_op jit(solution)/shard_map/ppermute | solution.py:20
  40.1 65.6 %collective-permute-start = (bf16[1024,768]{1,0:T(8,128)(2,1)}, bf16[1024,768]{1,0:T(8,128)(2,1)}, u32[]{:S(2)}, u32[]{:S(2)}) collective-permute-start(bf16[1024,768]{1,0:T(8,128)(2,1)} %pad_maximum_fusion.2), channel_id=1, source_target_pairs={{0,8},{8,16},{16,24},{24,32},{32,40},{40,48},{48,56},{56,64},{64,7... | collective-permute-start | bytes 4718600 | tf_op jit(solution)/shard_map/ppermute | solution.py:18
  43.7 45.9 %all-to-all-start = ((bf16[128,8,384]{0,2,1:T(8,128)(2,1)}), bf16[128,8,384]{0,2,1:T(8,128)(2,1)S(1)}, u32[]{:S(2)}, u32[]{:S(2)}) async-start(bf16[128,8,384]{0,2,1:T(8,128)(2,1)} %bitcast.25), calls=%async_computation | async-start | bytes 1572864 | tf_op jit(solution)/shard_map/all_to_all | solution.py:72
  89.6 13.6 %all-to-all-start.3 = ((bf16[128,8,384]{0,2,1:T(8,128)(2,1)}), bf16[128,8,384]{0,2,1:T(8,128)(2,1)S(1)}, u32[]{:S(2)}, u32[]{:S(2)}) async-start(bf16[128,8,384]{0,2,1:T(8,128)(2,1)} %bitcast.33), calls=%async_computation.3 | async-start | bytes 1572864 | tf_op jit(solution)/shard_map/all_to_all | solution.py:75
  117.4 4.8 copy-start.7
  139.7 2.3 copy-start.2
  139.7 3.7 copy-start.4
  142.0 2.9 copy-start.1
  145.0 5.6 %slice-start = ((s8[6291456]{0:T(1024)(128)(4,1)}), s8[2097152]{0:T(1024)(128)(4,1)S(1)}, s32[]{:S(2)}) async-start(s8[6291456]{0:T(1024)(128)(4,1)} %bitcast.147), calls=%async_computation.8 | async-start | bytes 4194304 | tf_op jit(solution)/shard_map/while
  145.1 5.5 %slice-start.1 = ((s8[6291456]{0:T(1024)(128)(4,1)}), s8[4194304]{0:T(1024)(128)(4,1)S(1)}, s32[]{:S(2)}) async-start(s8[6291456]{0:T(1024)(128)(4,1)} %bitcast.147), calls=%async_computation.9 | async-start | bytes 8388608 | tf_op jit(solution)/shard_map/while
  150.6 4.3 copy-start.3
  158.5 4.2 copy-start
  195.8 2.3 copy-start.2
  195.8 3.7 copy-start.4
  198.1 2.9 copy-start.1
  201.0 5.6 %slice-start = ((s8[6291456]{0:T(1024)(128)(4,1)}), s8[2097152]{0:T(1024)(128)(4,1)S(1)}, s32[]{:S(2)}) async-start(s8[6291456]{0:T(1024)(128)(4,1)} %bitcast.147), calls=%async_computation.8 | async-start | bytes 4194304 | tf_op jit(solution)/shard_map/while
  201.2 5.5 %slice-start.1 = ((s8[6291456]{0:T(1024)(128)(4,1)}), s8[4194304]{0:T(1024)(128)(4,1)S(1)}, s32[]{:S(2)}) async-start(s8[6291456]{0:T(1024)(128)(4,1)} %bitcast.147), calls=%async_computation.9 | async-start | bytes 8388608 | tf_op jit(solution)/shard_map/while
  206.7 4.3 copy-start.3
  214.6 4.2 copy-start
  251.7 2.3 copy-start.2
  251.8 3.7 copy-start.4
  254.1 2.9 copy-start.1
  257.0 5.6 %slice-start = ((s8[6291456]{0:T(1024)(128)(4,1)}), s8[2097152]{0:T(1024)(128)(4,1)S(1)}, s32[]{:S(2)}) async-start(s8[6291456]{0:T(1024)(128)(4,1)} %bitcast.147), calls=%async_computation.8 | async-start | bytes 4194304 | tf_op jit(solution)/shard_map/while
  257.2 5.5 %slice-start.1 = ((s8[6291456]{0:T(1024)(128)(4,1)}), s8[4194304]{0:T(1024)(128)(4,1)S(1)}, s32[]{:S(2)}) async-start(s8[6291456]{0:T(1024)(128)(4,1)} %bitcast.147), calls=%async_computation.9 | async-start | bytes 8388608 | tf_op jit(solution)/shard_map/while
  262.7 4.3 copy-start.3
  270.6 4.2 copy-start
  307.7 2.3 copy-start.2
  307.7 3.7 copy-start.4
  310.1 2.9 copy-start.1
  313.0 5.6 %slice-start = ((s8[6291456]{0:T(1024)(128)(4,1)}), s8[2097152]{0:T(1024)(128)(4,1)S(1)}, s32[]{:S(2)}) async-start(s8[6291456]{0:T(1024)(128)(4,1)} %bitcast.147), calls=%async_computation.8 | async-start | bytes 4194304 | tf_op jit(solution)/shard_map/while
  313.2 5.5 %slice-start.1 = ((s8[6291456]{0:T(1024)(128)(4,1)}), s8[4194304]{0:T(1024)(128)(4,1)S(1)}, s32[]{:S(2)}) async-start(s8[6291456]{0:T(1024)(128)(4,1)} %bitcast.147), calls=%async_computation.9 | async-start | bytes 8388608 | tf_op jit(solution)/shard_map/while
  318.6 4.3 copy-start.3
  326.6 4.2 copy-start
  346.4 12.4 %copy-start.6 = (bf16[4,256,384]{2,1,0:T(8,128)(2,1)S(1)}, bf16[4,256,384]{2,1,0:T(8,128)(2,1)}, u32[]{:S(2)}) copy-start(bf16[4,256,384]{2,1,0:T(8,128)(2,1)} %get-tuple-element.58) | copy-start | bytes 2359300
  353.1 97.1 %collective-permute-start.2 = (f32[1024,768]{0,1:T(8,128)}, f32[1024,768]{0,1:T(8,128)}, u32[]{:S(2)}, u32[]{:S(2)}) collective-permute-start(f32[1024,768]{0,1:T(8,128)} %get-tuple-element.149), channel_id=1, source_target_pairs={{8,0},{16,8},{24,16},{32,24},{40,32},{48,40},{56,48},{64,56},{72,6... | collective-permute-start | bytes 9437192 | tf_op jit(solution)/shard_map/ppermute | solution.py:30
  356.8 93.3 %collective-permute-start.3 = (f32[1024,768]{0,1:T(8,128)}, f32[1024,768]{0,1:T(8,128)}, u32[]{:S(2)}, u32[]{:S(2)}) collective-permute-start(f32[1024,768]{0,1:T(8,128)} %get-tuple-element.150), channel_id=1, source_target_pairs={{0,8},{8,16},{16,24},{24,32},{32,40},{40,48},{48,56},{56,64},{64,7... | collective-permute-start | bytes 9437192 | tf_op jit(solution)/shard_map/ppermute | solution.py:30
  444.6 15.7 %all-to-all-start.5 = ((bf16[8,128,384]{2,1,0:T(8,128)(2,1)}), bf16[8,128,384]{2,1,0:T(8,128)(2,1)S(1)}, u32[]{:S(2)}, u32[]{:S(2)}) async-start(bf16[8,128,384]{2,1,0:T(8,128)(2,1)} %bitcast.38), calls=%async_computation.5 | async-start | bytes 1572864 | tf_op jit(solution)/shard_map/all_to_all | solution.py:134
  460.3 13.6 %all-to-all-start.7 = ((bf16[8,128,384]{2,1,0:T(8,128)(2,1)}), bf16[8,128,384]{2,1,0:T(8,128)(2,1)S(1)}, u32[]{:S(2)}, u32[]{:S(2)}) async-start(bf16[8,128,384]{2,1,0:T(8,128)(2,1)} %bitcast.44), calls=%async_computation.7 | async-start | bytes 1572864 | tf_op jit(solution)/shard_map/all_to_all | solution.py:136
  473.9 13.6 %all-to-all-start.6 = ((bf16[8,128,384]{2,1,0:T(8,128)(2,1)}), bf16[8,128,384]{2,1,0:T(8,128)(2,1)S(1)}, u32[]{:S(2)}, u32[]{:S(2)}) async-start(bf16[8,128,384]{2,1,0:T(8,128)(2,1)} %bitcast.41), calls=%async_computation.6 | async-start | bytes 1572864 | tf_op jit(solution)/shard_map/all_to_all | solution.py:135
where the time goes:
time: 494 us; the launch traced here: 489 us
  local copies, waits for them, and re-layouts  97 us (20%)
  other arithmetic  96.9 us (20%)
  blocking collectives  85.9 us (17%)
  waiting for transfers between devices  84.1 us (17%)
  matrix products  65.3 us (13%)
  starting transfers between devices  38.3 us (8%)
  loops' own time  20.7 us (4%)
    all_to_all x1, blocking collectives, on_device(): lax.all_to_all(attended, 'heads', split_axis=0, concat_axis=1, tiled=True)  85.9 us
    dynamic_update_slice x32, other arithmetic, per_tile(): lax.dynamic_update_slice_in_dim(totals, current + grad_part[entry_pos * T...  71.6 us
    all_to_all x1, waiting for transfers between devices, on_device(): lax.all_to_all(queries, 'heads', split_axis=1, concat_axis=0, tiled=True)  40.1 us
    while x88, local copies, waits for them, and re-layouts  30 us
    dot_general x4, matrix products, tile_forward(): jnp.einsum('qhd,khd->hqk', grad_tile, value_sel, preferred_element_type=j...  21.7 us
    another operation x1, loops' own time, on_device(): lax.scan(per_tile, start_totals, (query_tiles, grad_tiles, key_tiles, key...  20.7 us
    dot_general x4, matrix products, key_side(): jnp.einsum('hqk,qhd->khd', weights_low, grad_tile, preferred_element_type...  17 us
    unnamed x14, local copies, waits for them, and re-layouts  13.9 us
  transfers between devices with their start and end apart: 11, of which 7 were waited for; matrix products, arithmetic and copies ran while one was open for 6% of the time, Pallas kernels for 0%

commit v1 on v0

v1 whole, which is shorter than its diff:
```python
import math

import jax
import jax.numpy as jnp
from jax import lax
from jax.experimental import pallas as pl
from jax.experimental.pallas import tpu as pltpu
from jax.sharding import PartitionSpec as P

HEAD_DIM = 128
TILE = 256
TILES_DEV = 4
ENTRIES = 8
NEAR = 3 * TILES_DEV
SLAB = TILES_DEV * TILE
SCALE = HEAD_DIM**-0.5
TO_LOG2 = SCALE * math.log2(math.e)
MASKED = -1e30
F32 = jnp.float32
BF16 = jnp.bfloat16
MESH = pl.DeviceIdType.MESH
ENTRY_ORDER = ((1, 0), (2, 0), (1, 1), (2, 1), (0, 0), (3, 0), (1, 2), (2, 2), (0, 1), (3, 1), (0, 2), (3, 2))
OFFSETS = ((0, 1), (1, 0), (3, 0), (2, 0), (1, 1), (3, 1), (2, 1))


def dot(a, b, a_dim, b_dim):
    return lax.dot_general(a, b, (((a_dim,), (b_dim,)), ((), ())), preferred_element_type=F32)


def tile_rows(tile):
    return pl.ds(pl.multiple_of(tile * TILE, TILE), TILE)


def flipped(index, flip):
    return index + flip * (1 - 2 * (index % 2))


def make_tables(base, key_tiles, key_count, slot_of, bias_of, entry_of):
    @pl.loop(0, TILES_DEV)
    def _(i):
        count = key_count[i]
        slots = [jnp.clip(key_tiles[i, e] - base, 0, NEAR - 1) for e in range(ENTRIES)]
        used = [(e < count).astype(jnp.int32) for e in range(ENTRIES)]
        firsts = []
        for e in range(ENTRIES):
            times = jnp.int32(0)
            before = jnp.int32(0)
            for other in range(ENTRIES):
                same = (slots[other] == slots[e]).astype(jnp.int32) * used[other]
                times = times + same
                if other < e:
                    before = before + same
            first = (before == 0).astype(jnp.int32) * used[e]
            bias = (1 - first).astype(F32) * MASKED
            for many in range(2, ENTRIES + 1):
                bias = bias + (first * (times == many).astype(jnp.int32)).astype(F32) * math.log2(many)
            firsts.append(first)
            slot_of[i, e] = slots[e]
            bias_of[i, e] = bias
        for j in range(NEAR):
            entry = jnp.int32(ENTRIES)
            for e in range(ENTRIES):
                entry = entry - (ENTRIES - e) * firsts[e] * (slots[e] == j).astype(jnp.int32)
            entry_of[i, j] = entry


def query_side(i, slot_of, bias_of, kw, vw, kt, vt, q, g, scores, weights, d_scores, g_low):
    best = jnp.full((8, TILE), -3e38, F32)
    for e in range(ENTRIES):
        s = dot(kw[slot_of[i, e]], q, 1, 1)
        scores[e] = s
        best = jnp.maximum(best, jnp.max(s.reshape(TILE // 8, 8, TILE), axis=0) + bias_of[i, e] * (1 / TO_LOG2))
    top = jnp.max(best, axis=0, keepdims=True) * TO_LOG2
    total = jnp.zeros((8, TILE), F32)
    out_t = jnp.zeros((HEAD_DIM, TILE), F32)
    for e in range(ENTRIES):
        p = jnp.exp2(scores[e] * TO_LOG2 - (top - bias_of[i, e]))
        total = total + jnp.sum(p.reshape(TILE // 8, 8, TILE), axis=0)
        p_low = p.astype(BF16)
        weights[i, e] = p_low
        out_t = out_t + dot(vt[slot_of[i, e]], p_low, 1, 0)
    inverse = 1.0 / jnp.sum(total, axis=0, keepdims=True)
    out_t = out_t * inverse
    g_t = (g.astype(F32).T * inverse).astype(BF16)
    g_low[i] = g_t
    row_dots = jnp.sum(g_t.astype(F32) * out_t, axis=0, keepdims=True)
    dq_t = jnp.zeros((HEAD_DIM, TILE), F32)
    for e in range(ENTRIES):
        dp = dot(vw[slot_of[i, e]], g_t, 1, 0)
        ds = (weights[i, e].astype(F32) * (dp - row_dots)).astype(BF16)
        d_scores[i, e] = ds
        dq_t = dq_t + dot(kt[slot_of[i, e]], ds, 1, 0)
    return out_t.T.astype(BF16), (dq_t * SCALE).T.astype(BF16)


def key_side(j, entry_of, q_of, weights, d_scores, g_low):
    dk = jnp.zeros((TILE, HEAD_DIM), F32)
    dv = jnp.zeros((TILE, HEAD_DIM), F32)
    for i in range(TILES_DEV):
        entry = entry_of[i, j]
        dk = dk + dot(d_scores[i, entry], q_of(i), 1, 0)
        dv = dv + dot(weights[i, entry], g_low[i], 1, 1)
    return dk * SCALE, dv


def kernel(
    frames, heads_dev, key_tiles, key_count, q_in, k_in, v_in, g_in, o_out, dq_out, dk_out, dv_out,
    slot_of, bias_of, entry_of, held, halo, grad_to, grad_from, leaving, kw, vw, kt, vt, scores, weights, d_scores, g_low,
    dk_own, dv_own, in_send, in_recv, halo_send, halo_recv, grad_send, grad_recv, out_send, out_recv,
):
    frame = lax.axis_index("frames")
    rank = lax.axis_index("heads")
    flip = (frame // 2) % 2
    row, side = rank // 2, rank % 2
    chunk = flipped(rank, flip)

    def partner(offset):
        return ((row + offset[0]) % 4) * 2 + (side + offset[1]) % 2

    neighbours = []
    for step in (frames - 1, 1):
        there = (frame + step) % frames
        neighbours.append({"frames": there, "heads": flipped(chunk, (there // 2) % 2)})

    barrier = pltpu.get_barrier_semaphore()
    for offset in OFFSETS:
        pl.semaphore_signal(barrier, inc=1, device_id={"frames": frame, "heads": partner(offset)}, device_id_type=MESH)
    for device in neighbours:
        pl.semaphore_signal(barrier, inc=1, device_id=device, device_id_type=MESH)
    pl.semaphore_wait(barrier, len(OFFSETS) + 2)

    def columns(of_chunk, h):
        return pl.ds(pl.multiple_of((of_chunk * heads_dev + h) * HEAD_DIM, HEAD_DIM), HEAD_DIM)

    def token_rows(of_rank):
        return pl.ds(pl.multiple_of(of_rank * 128, 128), 128)

    tensors = (q_in, k_in, v_in, g_in)
    outputs = (o_out, dq_out, dk_out, dv_out)

    for t, h in ENTRY_ORDER:
        for offset in OFFSETS:
            to = partner(offset)
            pltpu.make_async_remote_copy(
                src_ref=tensors[t].at[:, columns(flipped(to, flip), h)],
                dst_ref=held.at[t, h, token_rows(rank), :],
                send_sem=in_send.at[t, h],
                recv_sem=in_recv.at[t, h],
                device_id={"frames": frame, "heads": to},
                device_id_type=MESH,
            ).start()
        pltpu.make_async_copy(
            tensors[t].at[:, columns(chunk, h)], held.at[t, h, token_rows(rank), :], in_recv.at[t, h]
        ).start()

    def wait_bytes(ref, sem):
        pltpu.make_async_copy(ref, ref, sem).wait()

    def wait_in(t, h):
        wait_bytes(held.at[t, h], in_recv.at[t, h])

    def send_halo(h):
        for way in range(2):
            for kv in range(2):
                pltpu.make_async_remote_copy(
                    src_ref=held.at[1 + kv, h],
                    dst_ref=halo.at[h, 1 - way, kv],
                    send_sem=halo_send.at[h, way, kv],
                    recv_sem=halo_recv.at[h, 1 - way, kv],
                    device_id=neighbours[way],
                    device_id_type=MESH,
                ).start()

    def send_grads(h, way):
        for kv in range(2):
            pltpu.make_async_remote_copy(
                src_ref=grad_to.at[h, way, kv],
                dst_ref=grad_from.at[h, 1 - way, kv],
                send_sem=grad_send.at[h, way, kv],
                recv_sem=grad_recv.at[h, 1 - way, kv],
                device_id=neighbours[way],
                device_id_type=MESH,
            ).start()

    def send_out(t, h):
        for offset in OFFSETS:
            to = partner(offset)
            pltpu.make_async_remote_copy(
                src_ref=leaving.at[t, h, token_rows(to), :],
                dst_ref=outputs[t].at[:, columns(chunk, h)],
                send_sem=out_send.at[t, h],
                recv_sem=out_recv.at[t, h],
                device_id={"frames": frame, "heads": to},
                device_id_type=MESH,
            ).start()
        pltpu.make_async_copy(
            leaving.at[t, h, token_rows(rank), :], outputs[t].at[:, columns(chunk, h)], out_recv.at[t, h]
        ).start()

    make_tables((frame - 1) * TILES_DEV, key_tiles, key_count, slot_of, bias_of, entry_of)
    for i in range(TILES_DEV):
        weights[i, ENTRIES] = jnp.zeros((TILE, TILE), BF16)
        d_scores[i, ENTRIES] = jnp.zeros((TILE, TILE), BF16)

    for h in range(2):
        wait_in(1, h)
        wait_in(2, h)
        send_halo(h)

    def finish(h):
        for way in range(2):
            for kv in range(2):
                wait_bytes(grad_from.at[h, way, kv], grad_recv.at[h, way, kv])

        @pl.loop(0, TILES_DEV)
        def _(j):
            rows = tile_rows(j)
            for kv, own in ((0, dk_own), (1, dv_own)):
                whole = own[rows, :] + grad_from[h, 0, kv, rows, :].astype(F32) + grad_from[h, 1, kv, rows, :].astype(F32)
                leaving[2 + kv, h, rows, :] = whole.astype(BF16)

        send_out(2, h)
        send_out(3, h)

    @pl.loop(0, heads_dev)
    def _(h):
        wait_in(0, h)
        wait_in(3, h)
        for way in range(2):
            for kv in range(2):
                wait_bytes(halo.at[h, way, kv], halo_recv.at[h, way, kv])

        @pl.loop(0, TILES_DEV)
        def _(j):
            rows = tile_rows(j)
            for kv, flat, turned in ((0, kw, kt), (1, vw, vt)):
                for part, tile in enumerate((halo[h, 0, kv, rows, :], held[1 + kv, h, rows, :], halo[h, 1, kv, rows, :])):
                    flat[j + part * TILES_DEV] = tile
                    turned[j + part * TILES_DEV] = tile.T

        @pl.loop(0, TILES_DEV)
        def _(i):
            rows = tile_rows(i)
            out, dq = query_side(
                i, slot_of, bias_of, kw, vw, kt, vt, held[0, h, rows, :], held[3, h, rows, :], scores, weights, d_scores, g_low
            )
            leaving[0, h, rows, :] = out
            leaving[1, h, rows, :] = dq

        send_out(0, h)
        send_out(1, h)

        @pl.when(h == 0)
        def _():
            wait_in(1, 2)
            wait_in(2, 2)
            send_halo(2)

        @pl.when(h > 0)
        def _():
            finish(h - 1)

        def q_of(i):
            return held[0, h, i * TILE : (i + 1) * TILE, :]

        for way in (1, 0):
            @pl.loop(0, TILES_DEV)
            def _(j):
                dk, dv = key_side(j + way * 2 * TILES_DEV, entry_of, q_of, weights, d_scores, g_low)
                grad_to[h, way, 0, tile_rows(j), :] = dk.astype(BF16)
                grad_to[h, way, 1, tile_rows(j), :] = dv.astype(BF16)

            send_grads(h, way)

        @pl.loop(0, TILES_DEV)
        def _(j):
            dk, dv = key_side(j + TILES_DEV, entry_of, q_of, weights, d_scores, g_low)
            dk_own[tile_rows(j), :] = dk
            dv_own[tile_rows(j), :] = dv

    finish(heads_dev - 1)

    sent = SLAB - 128
    for h in range(heads_dev):
        for t in range(4):
            wait_bytes(held.at[t, h, 0:sent, :], in_send.at[t, h])
            wait_bytes(leaving.at[t, h, 0:sent, :], out_send.at[t, h])
            wait_bytes(leaving.at[t, h], out_recv.at[t, h])
        for way in range(2):
            for kv in range(2):
                wait_bytes(halo.at[h, way, kv], halo_send.at[h, way, kv])
                wait_bytes(grad_to.at[h, way, kv], grad_send.at[h, way, kv])


def on_device(queries, key_rows, value_rows, out_grad, key_tiles, key_count):
    frames = lax.axis_size("frames")
    tokens, features = queries.shape
    heads_dev = features // HEAD_DIM // lax.axis_size("heads")

    def body(*refs):
        kernel(frames, heads_dev, *refs)

    hbm = pl.BlockSpec(memory_space=pl.ANY)
    smem = pl.BlockSpec(memory_space=pltpu.SMEM)
    dma = pltpu.SemaphoreType.DMA
    return pl.pallas_call(
        body,
        out_shape=[jax.ShapeDtypeStruct((tokens, features), BF16)] * 4,
        in_specs=[smem, smem] + [hbm] * 4,
        out_specs=[hbm] * 4,
        scratch_shapes=[
            pltpu.SMEM((TILES_DEV, ENTRIES), jnp.int32),
            pltpu.SMEM((TILES_DEV, ENTRIES), F32),
            pltpu.SMEM((TILES_DEV, NEAR), jnp.int32),
            pltpu.VMEM((4, heads_dev, SLAB, HEAD_DIM), BF16),
            pltpu.VMEM((heads_dev, 2, 2, SLAB, HEAD_DIM), BF16),
            pltpu.VMEM((heads_dev, 2, 2, SLAB, HEAD_DIM), BF16),
            pltpu.VMEM((heads_dev, 2, 2, SLAB, HEAD_DIM), BF16),
            pltpu.VMEM((4, heads_dev, SLAB, HEAD_DIM), BF16),
            pltpu.VMEM((NEAR, TILE, HEAD_DIM), BF16),
            pltpu.VMEM((NEAR, TILE, HEAD_DIM), BF16),
            pltpu.VMEM((NEAR, HEAD_DIM, TILE), BF16),
            pltpu.VMEM((NEAR, HEAD_DIM, TILE), BF16),
            pltpu.VMEM((ENTRIES, TILE, TILE), F32),
            pltpu.VMEM((TILES_DEV, ENTRIES + 1, TILE, TILE), BF16),
            pltpu.VMEM((TILES_DEV, ENTRIES + 1, TILE, TILE), BF16),
            pltpu.VMEM((TILES_DEV, HEAD_DIM, TILE), BF16),
            pltpu.VMEM((SLAB, HEAD_DIM), F32),
            pltpu.VMEM((SLAB, HEAD_DIM), F32),
            dma((4, heads_dev)),
            dma((4, heads_dev)),
            dma((heads_dev, 2, 2)),
            dma((heads_dev, 2, 2)),
            dma((heads_dev, 2, 2)),
            dma((heads_dev, 2, 2)),
            dma((4, heads_dev)),
            dma((4, heads_dev)),
        ],
        compiler_params=pltpu.CompilerParams(collective_id=0, has_side_effects=True, vmem_limit_bytes=60 * 1024 * 1024),
        name="tile_attention",
    )(key_tiles, key_count, queries, key_rows, value_rows, out_grad)


def solution(mesh):
    spread = P(("frames", "heads"), None)
    return jax.shard_map(
        on_device,
        mesh=mesh,
        in_specs=(spread, spread, spread, spread, P("frames", None), P("frames")),
        out_specs=(spread, spread, spread, spread),
        check_vma=False,
    )
```

time: 494 us -> 111 us (0.22)
  Pallas kernels: 0 us -> 104 us
  other arithmetic: 96.9 us -> 0 us
  local copies, waits for them, and re-layouts: 97 us -> 5.85 us
  blocking collectives: 85.9 us -> 0 us
  waiting for transfers between devices: 84.1 us -> 0 us
  matrix products: 65.3 us -> 0 us
  starting transfers between devices: 38.3 us -> 0 us
  loops' own time: 20.7 us -> 0 us
    pallas_call x0 -> x1, Pallas kernels: none -> 104 us  [on_device(): pl.pallas_call(body, out_shape=[jax.ShapeDtypeStruct((tokens, features),...]
    all_to_all x1 -> x0, blocking collectives: 85.9 us -> none  [on_device(): lax.all_to_all(attended, 'heads', split_axis=0, concat_axis=1, tiled=True)]
    all_to_all x7 -> x0, waiting for transfers between devices: 84.1 us -> none  [the longest x1 40.1 us: on_device(): lax.all_to_all(queries, 'heads', split_axis=1, concat_axis=0, tiled=True)]
    dynamic_update_slice x32 -> x0, other arithmetic: 71.6 us -> none  [per_tile(): lax.dynamic_update_slice_in_dim(totals, current + grad_part[entry_pos * T...]
    dot_general x24 -> x0, matrix products: 65.3 us -> none  [the longest x4 21.7 us: tile_forward(): jnp.einsum('qhd,khd->hqk', grad_tile, value_sel, preferred_element_type=j...]
    while x91 -> x0, local copies, waits for them, and re-layouts: 39.6 us -> none
    all_to_all x7 -> x0, starting transfers between devices: 28.4 us -> none  [the longest x1 5.51 us: on_device(): lax.all_to_all(query_grad, 'heads', split_axis=0, concat_axis=1, tiled=True)]
    another operation x1 -> x0, loops' own time: 20.7 us -> none  [on_device(): lax.scan(per_tile, start_totals, (query_tiles, grad_tiles, key_tiles, key...]
  transfers between devices with their start and end apart: 11 -> 0, of which waited for: 7 -> 0; matrix products, arithmetic and copies ran while one was open for 6% -> 0% of each run, Pallas kernels for 0% -> 0%
where the time goes in v1:
time: 111 us
  Pallas kernels  104 us (94%)
  local copies, waits for them, and re-layouts  5.85 us (5%)
    pallas_call x1, Pallas kernels, on_device(): pl.pallas_call(body, out_shape=[jax.ShapeDtypeStruct((tokens, features),...  104 us
    unnamed x10, local copies, waits for them, and re-layouts  5.85 us

profile of v1, /device:TPU:100, one launch (start us, length us, event | category | flops | bytes accessed | tf_op | source)
XLA Modules:
  0.0 110.8 jit_solution(12053288339234801856)
XLA Ops:
  0.6 104.3 %tile_attention.1 = (bf16[128,3072]{1,0:T(8,128)(2,1)}, bf16[128,3072]{1,0:T(8,128)(2,1)}, bf16[128,3072]{1,0:T(8,128)(2,1)}, bf16[128,3072]{1,0:T(8,128)(2,1)}) custom-call(s32[4,8]{1,0:T(4,128)} %refs_0_.1, s32[4]{0:T(128)} %refs_1_.1, bf16[128,3072]{1,0:T(8,128)(2,1)} %refs_2_.1, bf16[128,3072]{1,0:T(8,128)(2,1)} %refs_3_.1, bf16[128,3072]{1,0:T(8,128)(2,1)} %refs_4_.1, ...), custom_call_target="tpu_custom_call" | custom-call | tf_op jit(solution)/shard_map/tile_attention/pallas_call | solution.py:306
  104.9 0.0 copy-start.2
  104.9 2.1 %copy.14 = bf16[128,3072]{1,0:T(8,128)(2,1)} copy(bf16[128,3072]{1,0:T(8,128)(2,1)} %get-tuple-element.8) | data formatting | bytes 1572864
  107.1 0.0 copy-done.2
  107.1 0.0 copy-start.1
  107.1 0.9 copy.15
  107.9 0.5 copy-done.1
  108.5 0.0 copy-start
  108.5 0.9 copy.16
  109.4 0.5 copy-done
  109.9 0.9 copy.17
Async XLA Ops:
  104.9 2.1 %copy-start.2 = (bf16[128,3072]{1,0:T(8,128)(2,1)S(1)}, bf16[128,3072]{1,0:T(8,128)(2,1)}, u32[]{:S(2)}) copy-start(bf16[128,3072]{1,0:T(8,128)(2,1)} %get-tuple-element.9) | copy-start | bytes 2359300
  107.1 1.4 %copy-start.1 = (bf16[128,3072]{1,0:T(8,128)(2,1)S(1)}, bf16[128,3072]{1,0:T(8,128)(2,1)}, u32[]{:S(2)}) copy-start(bf16[128,3072]{1,0:T(8,128)(2,1)} %get-tuple-element.10) | copy-start | bytes 2359300
  108.5 1.4 %copy-start = (bf16[128,3072]{1,0:T(8,128)(2,1)S(1)}, bf16[128,3072]{1,0:T(8,128)(2,1)}, u32[]{:S(2)}) copy-start(bf16[128,3072]{1,0:T(8,128)(2,1)} %get-tuple-element.11) | copy-start | bytes 2359300

commit v2 on v1

v2 whole, which is shorter than its diff:
```python
import math

import jax
import jax.numpy as jnp
from jax import lax
from jax.experimental import pallas as pl
from jax.experimental.pallas import tpu as pltpu
from jax.sharding import PartitionSpec as P

HEAD_DIM = 128
TILE = 256
TILES_DEV = 4
ENTRIES = 8
NEAR = 3 * TILES_DEV
WIDE = 5 * TILES_DEV
SLAB = TILES_DEV * TILE
SCALE = HEAD_DIM**-0.5
TO_LOG2 = SCALE * math.log2(math.e)
MASKED = -1e30
F32 = jnp.float32
BF16 = jnp.bfloat16
MESH = pl.DeviceIdType.MESH
OFFSETS = ((0, 1), (1, 0), (3, 0), (2, 0), (1, 1), (3, 1), (2, 1))


def dot(a, b, a_dim, b_dim):
    return lax.dot_general(a, b, (((a_dim,), (b_dim,)), ((), ())), preferred_element_type=F32)


def tile_rows(tile):
    return pl.ds(pl.multiple_of(tile * TILE, TILE), TILE)


def flipped(index, flip):
    return index + flip * (1 - 2 * (index % 2))


def make_tables(first_row, base, tiles_at, count_at, slot_of, bias_of, entry_of):
    @pl.loop(0, TILES_DEV)
    def _(i):
        count = count_at(i)
        slots = [jnp.clip(tiles_at(i, e) - base, 0, NEAR - 1) for e in range(ENTRIES)]
        used = [(e < count).astype(jnp.int32) for e in range(ENTRIES)]
        firsts = []
        for e in range(ENTRIES):
            times = jnp.int32(0)
            before = jnp.int32(0)
            for other in range(ENTRIES):
                same = (slots[other] == slots[e]).astype(jnp.int32) * used[other]
                times = times + same
                if other < e:
                    before = before + same
            first = (before == 0).astype(jnp.int32) * used[e]
            bias = (1 - first).astype(F32) * MASKED
            for many in range(2, ENTRIES + 1):
                bias = bias + (first * (times == many).astype(jnp.int32)).astype(F32) * math.log2(many)
            firsts.append(first)
            slot_of[first_row + i, e] = slots[e]
            bias_of[first_row + i, e] = bias
        for j in range(NEAR):
            entry = jnp.int32(ENTRIES)
            for e in range(ENTRIES):
                entry = entry - (ENTRIES - e) * firsts[e] * (slots[e] == j).astype(jnp.int32)
            entry_of[first_row + i, j] = entry


def query_side(table, first_tile, at, slot_of, bias_of, kw, vw, kt, vt, q, g, scores, weights, d_scores, g_low):
    best = jnp.full((8, TILE), -3e38, F32)
    for e in range(ENTRIES):
        s = dot(kw[first_tile + slot_of[table, e]], q, 1, 1)
        scores[e] = s
        best = jnp.maximum(best, jnp.max(s.reshape(TILE // 8, 8, TILE), axis=0) + bias_of[table, e] * (1 / TO_LOG2))
    top = jnp.max(best, axis=0, keepdims=True) * TO_LOG2
    total = jnp.zeros((8, TILE), F32)
    out_t = jnp.zeros((HEAD_DIM, TILE), F32)
    for e in range(ENTRIES):
        p = jnp.exp2(scores[e] * TO_LOG2 - (top - bias_of[table, e]))
        total = total + jnp.sum(p.reshape(TILE // 8, 8, TILE), axis=0)
        p_low = p.astype(BF16)
        weights[at, e] = p_low
        out_t = out_t + dot(vt[first_tile + slot_of[table, e]], p_low, 1, 0)
    inverse = 1.0 / jnp.sum(total, axis=0, keepdims=True)
    out_t = out_t * inverse
    g_t = (g.astype(F32).T * inverse).astype(BF16)
    g_low[at] = g_t
    row_dots = jnp.sum(g_t.astype(F32) * out_t, axis=0, keepdims=True)
    dq_t = jnp.zeros((HEAD_DIM, TILE), F32)
    for e in range(ENTRIES):
        dp = dot(vw[first_tile + slot_of[table, e]], g_t, 1, 0)
        ds = (weights[at, e].astype(F32) * (dp - row_dots)).astype(BF16)
        d_scores[at, e] = ds
        dq_t = dq_t + dot(kt[first_tile + slot_of[table, e]], ds, 1, 0)
    return out_t.T.astype(BF16), (dq_t * SCALE).T.astype(BF16)


def key_side(parts, entry_of, q_of, weights, d_scores, g_low):
    dk = jnp.zeros((TILE, HEAD_DIM), F32)
    dv = jnp.zeros((TILE, HEAD_DIM), F32)
    for table, at, task, j in parts:
        for i in range(TILES_DEV):
            entry = entry_of[table + i, j]
            dk = dk + dot(d_scores[at + i, entry], q_of(task, i), 1, 0)
            dv = dv + dot(weights[at + i, entry], g_low[at + i], 1, 1)
    return dk * SCALE, dv


def kernel(
    frames, key_tiles, key_count, q_in, k_in, v_in, g_in, o_out, dq_out, dk_out, dv_out,
    far_table, slot_of, bias_of, entry_of, table_to, table_from, held, near_a, near_b, to_a, from_a, to_b, from_b, leaving,
    kw, vw, kt, vt, scores, weights, d_scores, g_low, dk_own, dv_own,
    in_send, in_recv, near_a_send, near_a_recv, near_b_send, near_b_recv, to_a_send, from_a_recv, to_b_send, from_b_recv,
    out_send, out_extra, out_recv, table_sems,
):
    frame = lax.axis_index("frames")
    rank = lax.axis_index("heads")
    core = frame % 2
    half = (frame // 2) % 2
    plane = (frame // 4) * 4
    row, side = rank // 2, rank % 2
    pair = flipped(rank, half)
    whole_head = pair * 3 + 2 * half
    split_head = pair * 3 + 1

    def device(of_frame, of_rank):
        return {"frames": of_frame, "heads": of_rank}

    def partner(offset):
        return ((row + offset[0]) % 4) * 2 + (side + offset[1]) % 2

    def member(of_half):
        return plane + 2 * of_half + core

    twin = device(frame + 1 - 2 * core, rank)
    above = device((frame + frames - 3 + 6 * core) % frames, rank)
    neighbours = []
    for step in (frames - 1, 1):
        there = (frame + step) % frames
        neighbours.append(device(there, flipped(pair, (there // 2) % 2)))
    table_peer = device(member(1 - half), flipped(rank, 1))

    barrier = pltpu.get_barrier_semaphore()
    greeted = [device(frame, partner(offset)) for offset in OFFSETS]
    greeted += [device(member(1 - half), partner(offset)) for offset in OFFSETS + ((0, 0),)]
    greeted += neighbours + [above]
    for peer in greeted:
        pl.semaphore_signal(barrier, inc=1, device_id=peer, device_id_type=MESH)

    table = jnp.zeros((8, 128), jnp.int32)
    at_row = lax.broadcasted_iota(jnp.int32, (8, 128), 0)
    at_lane = lax.broadcasted_iota(jnp.int32, (8, 128), 1)
    for i in range(TILES_DEV):
        for e in range(ENTRIES):
            table = jnp.where((at_row == i) & (at_lane == e), key_tiles[i, e], table)
        table = jnp.where((at_row == i) & (at_lane == ENTRIES), key_count[i], table)
    table_to[...] = table

    pl.semaphore_wait(barrier, len(greeted))

    def columns(head):
        return pl.ds(pl.multiple_of(head * HEAD_DIM, HEAD_DIM), HEAD_DIM)

    def token_rows(of_rank):
        return pl.ds(pl.multiple_of(of_rank * 128, 128), 128)

    def send(src, dst, send_sem, recv_sem, to):
        pltpu.make_async_remote_copy(
            src_ref=src, dst_ref=dst, send_sem=send_sem, recv_sem=recv_sem, device_id=to, device_id_type=MESH
        ).start()

    def wait_bytes(ref, sem):
        pltpu.make_async_copy(ref, ref, sem).wait()

    tensors = (q_in, k_in, v_in, g_in)
    outputs = (o_out, dq_out, dk_out, dv_out)

    def enter_whole(t):
        here = held.at[t, half, token_rows(rank), :]
        for turn in range(2):
            of_half = (half + turn) % 2
            for offset in OFFSETS + ((0, 0),) * turn:
                to = partner(offset)
                head = flipped(to, of_half) * 3 + 2 * of_half
                send(tensors[t].at[:, columns(head)], here, in_send.at[t, turn], in_recv.at[t, half], device(member(of_half), to))
        pltpu.make_async_copy(tensors[t].at[:, columns(whole_head)], here, in_recv.at[t, half]).start()

    def enter_split(t):
        here = held.at[t, 2, token_rows(rank), :]
        for offset in OFFSETS:
            to = partner(offset)
            send(tensors[t].at[:, columns(flipped(to, half) * 3 + 1)], here, in_send.at[t, 2], in_recv.at[t, 2], device(frame, to))
        pltpu.make_async_copy(tensors[t].at[:, columns(split_head)], here, in_recv.at[t, 2]).start()

    def leave_whole(t, task):
        there = outputs[t].at[:, columns(whole_head)]
        turn = (task + half) % 2
        for offset in OFFSETS:
            to = partner(offset)
            send(leaving.at[t, task, token_rows(to), :], there, out_send.at[t, task], out_recv.at[t, turn], device(member(task), to))

        @pl.when(turn == 0)
        def _():
            pltpu.make_async_copy(leaving.at[t, task, token_rows(rank), :], there, out_recv.at[t, 0]).start()

        @pl.when(turn == 1)
        def _():
            send(leaving.at[t, task, token_rows(rank), :], there, out_extra.at[t], out_recv.at[t, 1], device(member(1 - half), rank))

    def leave_split(t):
        there = outputs[t].at[:, columns(split_head)]
        for offset in OFFSETS:
            to = partner(offset)
            send(leaving.at[t, 2, token_rows(to), :], there, out_send.at[t, 2], out_recv.at[t, 2], device(frame, to))
        pltpu.make_async_copy(leaving.at[t, 2, token_rows(rank), :], there, out_recv.at[t, 2]).start()

    def wait_in(t, task):
        wait_bytes(held.at[t, task], in_recv.at[t, task])

    send(table_to, table_from, table_sems.at[0], table_sems.at[1], table_peer)
    for t in (1, 2, 0, 3):
        enter_whole(t)
    for t in (1, 2, 0, 3):
        enter_split(t)

    make_tables(
        half * TILES_DEV, (frame - 1) * TILES_DEV, lambda i, e: key_tiles[i, e], lambda i: key_count[i], slot_of, bias_of, entry_of
    )
    wait_bytes(table_from, table_sems.at[1])
    pltpu.make_async_copy(table_from, far_table, table_sems.at[2]).start()
    for i in range(2 * TILES_DEV):
        weights[i, ENTRIES] = jnp.zeros((TILE, TILE), BF16)
        d_scores[i, ENTRIES] = jnp.zeros((TILE, TILE), BF16)
    pltpu.make_async_copy(table_from, far_table, table_sems.at[2]).wait()
    make_tables(
        (1 - half) * TILES_DEV, (member(1 - half) - 1) * TILES_DEV,
        lambda i, e: far_table[i, e], lambda i: far_table[i, ENTRIES], slot_of, bias_of, entry_of,
    )

    for kv in range(2):
        for task in range(2):
            wait_in(1 + kv, task)
            send(
                held.at[1 + kv, task], near_a.at[task + core, kv], near_a_send.at[task, kv], near_a_recv.at[task, kv], twin
            )
        send(held.at[1 + kv, core], near_a.at[2 - 2 * core, kv], near_a_send.at[2, kv], near_a_recv.at[2, kv], above)

    def spread(tile, kv, block):
        (kw, vw)[kv][tile] = block
        (kt, vt)[kv][tile] = block.T

    @pl.loop(0, TILES_DEV)
    def _(j):
        for kv in range(2):
            for task in range(2):
                spread((2 * task + 1) * TILES_DEV + j, kv, held[1 + kv, task, tile_rows(j), :])

    def take_near(slot, sem):
        for kv in range(2):
            wait_bytes(near_a.at[slot, kv], near_a_recv.at[sem, kv])

        @pl.loop(0, TILES_DEV)
        def _(j):
            for kv in range(2):
                spread(2 * slot * TILES_DEV + j, kv, near_a[slot, kv, tile_rows(j), :])

    for task in range(2):
        take_near(task + 1 - core, task)

    def queries(task, table, first_tile, at):
        @pl.loop(0, TILES_DEV)
        def _(i):
            rows = tile_rows(i)
            out, dq = query_side(
                table + i, first_tile, at + i, slot_of, bias_of, kw, vw, kt, vt,
                held[0, task, rows, :], held[3, task, rows, :], scores, weights, d_scores, g_low,
            )
            leaving[0, task, rows, :] = out
            leaving[1, task, rows, :] = dq

    def q_of(task, i):
        return held[0, task, i * TILE : (i + 1) * TILE, :]

    def keys(put, *parts):
        @pl.loop(0, TILES_DEV)
        def _(j):
            dk, dv = key_side(
                [(table, at, task, j + part * TILES_DEV) for table, at, task, part in parts],
                entry_of, q_of, weights, d_scores, g_low,
            )
            put(tile_rows(j), dk, dv)

    def to_near(slot):
        def put(rows, dk, dv):
            to_a[slot, 0, rows, :] = dk.astype(BF16)
            to_a[slot, 1, rows, :] = dv.astype(BF16)

        return put

    def to_own(task):
        def put(rows, dk, dv):
            dk_own[task, rows, :] = dk
            dv_own[task, rows, :] = dv

        return put

    def whole_parts(task, part):
        return (task * TILES_DEV, task * TILES_DEV, task, part)

    def hand_over(slot, sem, at, to):
        for kv in range(2):
            send(to_a.at[slot, kv], from_a.at[at, kv], to_a_send.at[sem, kv], from_a_recv.at[at, kv], to)

    first, second = 1 - core, core
    wait_in(0, first)
    wait_in(3, first)
    queries(first, first * TILES_DEV, 2 * first * TILES_DEV, first * TILES_DEV)
    leave_whole(0, first)
    leave_whole(1, first)
    keys(to_near(2 * first), whole_parts(first, 2 * first))
    hand_over(2 * first, 0, first, twin)
    keys(to_own(first), whole_parts(first, 1))

    for kv in range(2):
        wait_in(1 + kv, 2)
        for way in range(2):
            send(
                held.at[1 + kv, 2], near_b.at[1 - way, kv], near_b_send.at[way, kv], near_b_recv.at[1 - way, kv], neighbours[way]
            )

    take_near(2 * core, 2)
    wait_in(0, second)
    wait_in(3, second)
    queries(second, second * TILES_DEV, 2 * second * TILES_DEV, second * TILES_DEV)
    leave_whole(0, second)
    leave_whole(1, second)
    keys(to_near(2 * second), whole_parts(second, 2 * second))
    hand_over(2 * second, 1, 2, above)
    keys(to_near(1), whole_parts(0, 2), whole_parts(1, 0))
    hand_over(1, 2, second, twin)
    keys(to_own(second), whole_parts(second, 1))

    wait_in(0, 2)
    wait_in(3, 2)
    for way in range(2):
        for kv in range(2):
            wait_bytes(near_b.at[way, kv], near_b_recv.at[way, kv])

    @pl.loop(0, TILES_DEV)
    def _(j):
        for kv in range(2):
            spread(j, kv, near_b[0, kv, tile_rows(j), :])
            spread(TILES_DEV + j, kv, held[1 + kv, 2, tile_rows(j), :])
            spread(2 * TILES_DEV + j, kv, near_b[1, kv, tile_rows(j), :])

    queries(2, half * TILES_DEV, 0, 0)
    leave_split(0)
    leave_split(1)

    for at in range(3):
        for kv in range(2):
            wait_bytes(from_a.at[at, kv], from_a_recv.at[at, kv])

    for task in range(2):
        border = (core == task).astype(F32)

        @pl.loop(0, TILES_DEV)
        def _(j):
            rows = tile_rows(j)
            for kv, own in ((0, dk_own), (1, dv_own)):
                total = own[task, rows, :] + from_a[task, kv, rows, :].astype(F32)
                total = total + border * from_a[2, kv, rows, :].astype(F32)
                leaving[2 + kv, task, rows, :] = total.astype(BF16)

        leave_whole(2, task)
        leave_whole(3, task)

    for way in (0, 1):
        def put(rows, dk, dv):
            to_b[way, 0, rows, :] = dk.astype(BF16)
            to_b[way, 1, rows, :] = dv.astype(BF16)

        keys(put, (half * TILES_DEV, 0, 2, 2 * way))
        for kv in range(2):
            send(to_b.at[way, kv], from_b.at[1 - way, kv], to_b_send.at[way, kv], from_b_recv.at[1 - way, kv], neighbours[way])
    keys(to_own(0), (half * TILES_DEV, 0, 2, 1))

    for kv, own in ((0, dk_own), (1, dv_own)):
        for way in range(2):
            wait_bytes(from_b.at[way, kv], from_b_recv.at[way, kv])

        @pl.loop(0, TILES_DEV)
        def _(j):
            rows = tile_rows(j)
            total = own[0, rows, :] + from_b[0, kv, rows, :].astype(F32) + from_b[1, kv, rows, :].astype(F32)
            leaving[2 + kv, 2, rows, :] = total.astype(BF16)

        leave_split(2 + kv)

    seven = SLAB - 128
    for t in range(4):
        wait_bytes(held.at[t, 0, 0:seven, :], in_send.at[t, 0])
        wait_bytes(held.at[t, 0], in_send.at[t, 1])
        wait_bytes(held.at[t, 0, 0:seven, :], in_send.at[t, 2])
        wait_bytes(leaving.at[t, 0, 0:128, :], out_extra.at[t])
        for task in range(3):
            wait_bytes(leaving.at[t, task, 0:seven, :], out_send.at[t, task])
            wait_bytes(leaving.at[t, task], out_recv.at[t, task])
    for kv in range(2):
        for at in range(3):
            wait_bytes(near_a.at[at, kv], near_a_send.at[at, kv])
            wait_bytes(to_a.at[at, kv], to_a_send.at[at, kv])
        for way in range(2):
            wait_bytes(near_b.at[way, kv], near_b_send.at[way, kv])
            wait_bytes(to_b.at[way, kv], to_b_send.at[way, kv])
    wait_bytes(table_to, table_sems.at[0])


def on_device(queries, key_rows, value_rows, out_grad, key_tiles, key_count):
    frames = lax.axis_size("frames")
    tokens, features = queries.shape

    def body(*refs):
        kernel(frames, *refs)

    hbm = pl.BlockSpec(memory_space=pl.ANY)
    smem = pl.BlockSpec(memory_space=pltpu.SMEM)
    dma = pltpu.SemaphoreType.DMA
    block = (SLAB, HEAD_DIM)
    return pl.pallas_call(
        body,
        out_shape=[jax.ShapeDtypeStruct((tokens, features), BF16)] * 4,
        in_specs=[smem, smem] + [hbm] * 4,
        out_specs=[hbm] * 4,
        scratch_shapes=[
            pltpu.SMEM((8, 128), jnp.int32),
            pltpu.SMEM((2 * TILES_DEV, ENTRIES), jnp.int32),
            pltpu.SMEM((2 * TILES_DEV, ENTRIES), F32),
            pltpu.SMEM((2 * TILES_DEV, NEAR), jnp.int32),
            pltpu.VMEM((8, 128), jnp.int32),
            pltpu.VMEM((8, 128), jnp.int32),
            pltpu.VMEM((4, 3) + block, BF16),
            pltpu.VMEM((3, 2) + block, BF16),
            pltpu.VMEM((2, 2) + block, BF16),
            pltpu.VMEM((3, 2) + block, BF16),
            pltpu.VMEM((3, 2) + block, BF16),
            pltpu.VMEM((2, 2) + block, BF16),
            pltpu.VMEM((2, 2) + block, BF16),
            pltpu.VMEM((4, 3) + block, BF16),
            pltpu.VMEM((WIDE, TILE, HEAD_DIM), BF16),
            pltpu.VMEM((WIDE, TILE, HEAD_DIM), BF16),
            pltpu.VMEM((WIDE, HEAD_DIM, TILE), BF16),
            pltpu.VMEM((WIDE, HEAD_DIM, TILE), BF16),
            pltpu.VMEM((ENTRIES, TILE, TILE), F32),
            pltpu.VMEM((2 * TILES_DEV, ENTRIES + 1, TILE, TILE), BF16),
            pltpu.VMEM((2 * TILES_DEV, ENTRIES + 1, TILE, TILE), BF16),
            pltpu.VMEM((2 * TILES_DEV, HEAD_DIM, TILE), BF16),
            pltpu.VMEM((2,) + block, F32),
            pltpu.VMEM((2,) + block, F32),
            dma((4, 3)),
            dma((4, 3)),
            dma((3, 2)),
            dma((3, 2)),
            dma((2, 2)),
            dma((2, 2)),
            dma((3, 2)),
            dma((3, 2)),
            dma((2, 2)),
            dma((2, 2)),
            dma((4, 3)),
            dma((4,)),
            dma((4, 3)),
            dma((3,)),
        ],
        compiler_params=pltpu.CompilerParams(collective_id=0, has_side_effects=True, vmem_limit_bytes=60 * 1024 * 1024),
        name="tile_attention",
    )(key_tiles, key_count, queries, key_rows, value_rows, out_grad)


def solution(mesh):
    spread = P(("frames", "heads"), None)
    return jax.shard_map(
        on_device,
        mesh=mesh,
        in_specs=(spread, spread, spread, spread, P("frames", None), P("frames")),
        out_specs=(spread, spread, spread, spread),
        check_vma=False,
    )
```

time: 111 us -> 111 us (level); the launches traced: 111 us -> 109 us
    pallas_call x1, Pallas kernels: 104 us -> 103 us  [on_device(): pl.pallas_call(body, out_shape=[jax.ShapeDtypeStruct((tokens, features),...]
where the time goes in v2:
time: 111 us; the launch traced here: 109 us
  Pallas kernels  103 us (93%)
  local copies, waits for them, and re-layouts  5.85 us (5%)
    pallas_call x1, Pallas kernels, on_device(): pl.pallas_call(body, out_shape=[jax.ShapeDtypeStruct((tokens, features),...  103 us
    unnamed x10, local copies, waits for them, and re-layouts  5.85 us

profile of v2, /device:TPU:100, one launch (start us, length us, event | category | flops | bytes accessed | tf_op | source)
XLA Modules:
  0.0 109.3 jit_solution(10507749781942463539)
XLA Ops:
  0.6 102.8 %tile_attention.1 = (bf16[128,3072]{1,0:T(8,128)(2,1)}, bf16[128,3072]{1,0:T(8,128)(2,1)}, bf16[128,3072]{1,0:T(8,128)(2,1)}, bf16[128,3072]{1,0:T(8,128)(2,1)}) custom-call(s32[4,8]{1,0:T(4,128)} %refs_0_.1, s32[4]{0:T(128)} %refs_1_.1, bf16[128,3072]{1,0:T(8,128)(2,1)} %refs_2_.1, bf16[128,3072]{1,0:T(8,128)(2,1)} %refs_3_.1, bf16[128,3072]{1,0:T(8,128)(2,1)} %refs_4_.1, ...), custom_call_target="tpu_custom_call" | custom-call | tf_op jit(solution)/shard_map/tile_attention/pallas_call | solution.py:428
  103.4 0.0 copy-start.2
  103.4 2.1 %copy.14 = bf16[128,3072]{1,0:T(8,128)(2,1)} copy(bf16[128,3072]{1,0:T(8,128)(2,1)} %get-tuple-element.8) | data formatting | bytes 1572864
  105.5 0.0 copy-done.2
  105.5 0.0 copy-start.1
  105.5 0.9 copy.15
  106.4 0.5 copy-done.1
  107.0 0.0 copy-start
  107.0 0.9 copy.16
  107.8 0.5 copy-done
  108.4 0.9 copy.17
Async XLA Ops:
  103.4 2.1 %copy-start.2 = (bf16[128,3072]{1,0:T(8,128)(2,1)S(1)}, bf16[128,3072]{1,0:T(8,128)(2,1)}, u32[]{:S(2)}) copy-start(bf16[128,3072]{1,0:T(8,128)(2,1)} %get-tuple-element.9) | copy-start | bytes 2359300
  105.5 1.4 %copy-start.1 = (bf16[128,3072]{1,0:T(8,128)(2,1)S(1)}, bf16[128,3072]{1,0:T(8,128)(2,1)}, u32[]{:S(2)}) copy-start(bf16[128,3072]{1,0:T(8,128)(2,1)} %get-tuple-element.10) | copy-start | bytes 2359300
  107.0 1.4 %copy-start = (bf16[128,3072]{1,0:T(8,128)(2,1)S(1)}, bf16[128,3072]{1,0:T(8,128)(2,1)}, u32[]{:S(2)}) copy-start(bf16[128,3072]{1,0:T(8,128)(2,1)} %get-tuple-element.11) | copy-start | bytes 2359300

commit v3 on v2

--- a/solution.py
+++ b/solution.py
@@ -17,6 +17,7 @@
 SCALE = HEAD_DIM**-0.5
 TO_LOG2 = SCALE * math.log2(math.e)
 MASKED = -1e30
+PIECE = 32
 F32 = jnp.float32
 BF16 = jnp.bfloat16
 MESH = pl.DeviceIdType.MESH
@@ -64,21 +65,26 @@
             entry_of[first_row + i, j] = entry
 
 
-def query_side(table, first_tile, at, slot_of, bias_of, kw, vw, kt, vt, q, g, scores, weights, d_scores, g_low):
-    best = jnp.full((8, TILE), -3e38, F32)
-    for e in range(ENTRIES):
-        s = dot(kw[first_tile + slot_of[table, e]], q, 1, 1)
-        scores[e] = s
-        best = jnp.maximum(best, jnp.max(s.reshape(TILE // 8, 8, TILE), axis=0) + bias_of[table, e] * (1 / TO_LOG2))
+def score(e, table, first_tile, slot_of, bias_of, kw, q, scores, best):
+    s = dot(kw[first_tile + slot_of[table, e]], q, 1, 1)
+    scores[e] = s
+    return jnp.maximum(best, jnp.max(s.reshape(TILE // 8, 8, TILE), axis=0) + bias_of[table, e] * (1 / TO_LOG2))
+
+
+def query_side(table, first_tile, at, slot_of, bias_of, vw, kt, vt, g, scores, weights, d_scores, g_low, best, score_next):
     top = jnp.max(best, axis=0, keepdims=True) * TO_LOG2
     total = jnp.zeros((8, TILE), F32)
     out_t = jnp.zeros((HEAD_DIM, TILE), F32)
+    best_next = no_best()
     for e in range(ENTRIES):
-        p = jnp.exp2(scores[e] * TO_LOG2 - (top - bias_of[table, e]))
-        total = total + jnp.sum(p.reshape(TILE // 8, 8, TILE), axis=0)
-        p_low = p.astype(BF16)
-        weights[at, e] = p_low
-        out_t = out_t + dot(vt[first_tile + slot_of[table, e]], p_low, 1, 0)
+        offset = top - bias_of[table, e]
+        best_next = score_next(e, best_next)
+        for part in range(TILE // PIECE):
+            rows = slice(part * PIECE, (part + 1) * PIECE)
+            p = jnp.exp2(scores[e, rows, :] * TO_LOG2 - offset)
+            total = total + jnp.sum(p.reshape(PIECE // 8, 8, TILE), axis=0)
+            weights[at, e, rows, :] = p.astype(BF16)
+        out_t = out_t + dot(vt[first_tile + slot_of[table, e]], weights[at, e], 1, 0)
     inverse = 1.0 / jnp.sum(total, axis=0, keepdims=True)
     out_t = out_t * inverse
     g_t = (g.astype(F32).T * inverse).astype(BF16)
@@ -90,7 +96,11 @@
         ds = (weights[at, e].astype(F32) * (dp - row_dots)).astype(BF16)
         d_scores[at, e] = ds
         dq_t = dq_t + dot(kt[first_tile + slot_of[table, e]], ds, 1, 0)
-    return out_t.T.astype(BF16), (dq_t * SCALE).T.astype(BF16)
+    return out_t.T.astype(BF16), (dq_t * SCALE).T.astype(BF16), best_next
+
+
+def no_best():
+    return jnp.full((8, TILE), -3e38, F32)
 
 
 def key_side(parts, entry_of, q_of, weights, d_scores, g_low):
@@ -98,16 +108,17 @@
     dv = jnp.zeros((TILE, HEAD_DIM), F32)
     for table, at, task, j in parts:
         for i in range(TILES_DEV):
-            entry = entry_of[table + i, j]
-            dk = dk + dot(d_scores[at + i, entry], q_of(task, i), 1, 0)
-            dv = dv + dot(weights[at + i, entry], g_low[at + i], 1, 1)
+            dk = dk + dot(d_scores[at + i, entry_of[table + i, j]], q_of(task, i), 1, 0)
+    for table, at, task, j in parts:
+        for i in range(TILES_DEV):
+            dv = dv + dot(weights[at + i, entry_of[table + i, j]], g_low[at + i], 1, 1)
     return dk * SCALE, dv
 
 
 def kernel(
     frames, key_tiles, key_count, q_in, k_in, v_in, g_in, o_out, dq_out, dk_out, dv_out,
     far_table, slot_of, bias_of, entry_of, table_to, table_from, held, near_a, near_b, to_a, from_a, to_b, from_b, leaving,
-    kw, vw, kt, vt, scores, weights, d_scores, g_low, dk_own, dv_own,
+    kw, vw, kt, vt, scores_even, scores_odd, weights, d_scores, g_low, dk_own, dv_own,
     in_send, in_recv, near_a_send, near_a_recv, near_b_send, near_b_recv, to_a_send, from_a_recv, to_b_send, from_b_recv,
     out_send, out_extra, out_recv, table_sems,
 ):
@@ -216,10 +227,25 @@
         wait_bytes(held.at[t, task], in_recv.at[t, task])
 
     send(table_to, table_from, table_sems.at[0], table_sems.at[1], table_peer)
-    for t in (1, 2, 0, 3):
-        enter_whole(t)
-    for t in (1, 2, 0, 3):
-        enter_split(t)
+    first, second = 1 - core, core
+    enter_whole(1)
+    enter_whole(2)
+
+    @pl.when(half == first)
+    def _():
+        enter_whole(0)
+        enter_whole(3)
+
+    enter_split(1)
+    enter_split(2)
+
+    @pl.when(half == second)
+    def _():
+        enter_whole(0)
+        enter_whole(3)
+
+    enter_split(0)
+    enter_split(3)
 
     make_tables(
         half * TILES_DEV, (frame - 1) * TILES_DEV, lambda i, e: key_tiles[i, e], lambda i: key_count[i], slot_of, bias_of, entry_of
@@ -266,21 +292,36 @@
         take_near(task + 1 - core, task)
 
     def queries(task, table, first_tile, at):
-        @pl.loop(0, TILES_DEV)
-        def _(i):
+        def score_of(i, scores):
+            def one(e, best):
+                return score(e, table + i, first_tile, slot_of, bias_of, kw, held[0, task, tile_rows(i), :], scores, best)
+
+            return one
+
+        def tile(i, scores, best, score_next):
             rows = tile_rows(i)
-            out, dq = query_side(
-                table + i, first_tile, at + i, slot_of, bias_of, kw, vw, kt, vt,
-                held[0, task, rows, :], held[3, task, rows, :], scores, weights, d_scores, g_low,
+            out, dq, best = query_side(
+                table + i, first_tile, at + i, slot_of, bias_of, vw, kt, vt, held[3, task, rows, :],
+                scores, weights, d_scores, g_low, best, score_next,
             )
             leaving[0, task, rows, :] = out
             leaving[1, task, rows, :] = dq
+            return best
+
+        def two(k, best):
+            best = tile(2 * k, scores_even, best, score_of(2 * k + 1, scores_odd))
+            return tile(2 * k + 1, scores_odd, best, score_of((2 * k + 2) % TILES_DEV, scores_even))
+
+        best = no_best()
+        for e in range(ENTRIES):
+            best = score_of(0, scores_even)(e, best)
+        lax.fori_loop(0, TILES_DEV // 2, two, best)
 
     def q_of(task, i):
         return held[0, task, i * TILE : (i + 1) * TILE, :]
 
     def keys(put, *parts):
-        @pl.loop(0, TILES_DEV)
+        @pl.loop(0, TILES_DEV, unroll=2)
         def _(j):
             dk, dv = key_side(
                 [(table, at, task, j + part * TILES_DEV) for table, at, task, part in parts],
@@ -309,7 +350,6 @@
         for kv in range(2):
             send(to_a.at[slot, kv], from_a.at[at, kv], to_a_send.at[sem, kv], from_a_recv.at[at, kv], to)
 
-    first, second = 1 - core, core
     wait_in(0, first)
     wait_in(3, first)
     queries(first, first * TILES_DEV, 2 * first * TILES_DEV, first * TILES_DEV)
@@ -414,6 +454,19 @@
     wait_bytes(table_to, table_sems.at[0])
 
 
+def copy_out(*refs):
+    sources, results, pieces, sems = refs[:4], refs[4:8], refs[8], refs[9]
+    inward = [pltpu.make_async_copy(sources[t], pieces.at[t], sems.at[0, t]) for t in range(4)]
+    outward = [pltpu.make_async_copy(pieces.at[t], results[t], sems.at[1, t]) for t in range(4)]
+    for copy in inward:
+        copy.start()
+    for t in range(4):
+        inward[t].wait()
+        outward[t].start()
+    for copy in outward:
+        copy.wait()
+
+
 def on_device(queries, key_rows, value_rows, out_grad, key_tiles, key_count):
     frames = lax.axis_size("frames")
     tokens, features = queries.shape
@@ -425,9 +478,10 @@
     smem = pl.BlockSpec(memory_space=pltpu.SMEM)
     dma = pltpu.SemaphoreType.DMA
     block = (SLAB, HEAD_DIM)
-    return pl.pallas_call(
+    shapes = [jax.ShapeDtypeStruct((tokens, features), BF16)] * 4
+    results = pl.pallas_call(
         body,
-        out_shape=[jax.ShapeDtypeStruct((tokens, features), BF16)] * 4,
+        out_shape=shapes,
         in_specs=[smem, smem] + [hbm] * 4,
         out_specs=[hbm] * 4,
         scratch_shapes=[
@@ -449,6 +503,7 @@
             pltpu.VMEM((WIDE, TILE, HEAD_DIM), BF16),
             pltpu.VMEM((WIDE, HEAD_DIM, TILE), BF16),
             pltpu.VMEM((WIDE, HEAD_DIM, TILE), BF16),
+            pltpu.VMEM((ENTRIES, TILE, TILE), F32),
             pltpu.VMEM((ENTRIES, TILE, TILE), F32),
             pltpu.VMEM((2 * TILES_DEV, ENTRIES + 1, TILE, TILE), BF16),
             pltpu.VMEM((2 * TILES_DEV, ENTRIES + 1, TILE, TILE), BF16),
@@ -473,6 +528,14 @@
         compiler_params=pltpu.CompilerParams(collective_id=0, has_side_effects=True, vmem_limit_bytes=60 * 1024 * 1024),
         name="tile_attention",
     )(key_tiles, key_count, queries, key_rows, value_rows, out_grad)
+    return pl.pallas_call(
+        copy_out,
+        out_shape=shapes,
+        in_specs=[hbm] * 4,
+        out_specs=[hbm] * 4,
+        scratch_shapes=[pltpu.VMEM((4, tokens, features), BF16), dma((2, 4))],
+        name="copy_out",
+    )(*results)
 
 
 def solution(mesh):

time: 111 us -> 100 us (0.901)
  local copies, waits for them, and re-layouts: 5.85 us -> 0 us
  Pallas kernels: 103 us -> 98.3 us
    unnamed x10 -> x0, local copies, waits for them, and re-layouts: 5.85 us -> none
    pallas_call x1 -> x2, Pallas kernels: 103 us -> 98.3 us  [the longest x1 95.4 us: on_device(): pl.pallas_call(body, out_shape=shapes, in_specs=[smem, smem] + [hbm] * 4,...]
where the time goes in v3:
time: 100 us; the launch traced here: 99.1 us
  Pallas kernels  98.3 us (98%)
    pallas_call x1, Pallas kernels, on_device(): pl.pallas_call(body, out_shape=shapes, in_specs=[smem, smem] + [hbm] * 4,...  95.4 us
    pallas_call x1, Pallas kernels, on_device(): pl.pallas_call(copy_out, out_shape=shapes, in_specs=[hbm] * 4, out_specs=...  2.86 us

profile of v3, /device:TPU:100, one launch (start us, length us, event | category | flops | bytes accessed | tf_op | source)
XLA Modules:
  0.0 99.1 jit_solution(14802527632238819231)
XLA Ops:
  0.6 95.4 %tile_attention.1 = (bf16[128,3072]{1,0:T(8,128)(2,1)}, bf16[128,3072]{1,0:T(8,128)(2,1)}, bf16[128,3072]{1,0:T(8,128)(2,1)}, bf16[128,3072]{1,0:T(8,128)(2,1)}) custom-call(s32[4,8]{1,0:T(4,128)} %refs_0_.1, s32[4]{0:T(128)} %refs_1_.1, bf16[128,3072]{1,0:T(8,128)(2,1)} %refs_2_.1, bf16[128,3072]{1,0:T(8,128)(2,1)} %refs_3_.1, bf16[128,3072]{1,0:T(8,128)(2,1)} %refs_4_.1, ...), custom_call_target="tpu_custom_call" | custom-call | tf_op jit(solution)/shard_map/tile_attention/pallas_call | solution.py:482
  96.1 2.9 %copy_out.1 = (bf16[128,3072]{1,0:T(8,128)(2,1)}, bf16[128,3072]{1,0:T(8,128)(2,1)}, bf16[128,3072]{1,0:T(8,128)(2,1)}, bf16[128,3072]{1,0:T(8,128)(2,1)}) custom-call(bf16[128,3072]{1,0:T(8,128)(2,1)} %get-tuple-element.8.refs_0_, bf16[128,3072]{1,0:T(8,128)(2,1)} %get-tuple-element.9.refs_1_, bf16[128,3072]{1,0:T(8,128)(2,1)} %get-tuple-element.10.refs_2_, ...), custom_call_target="tpu_custom_call" | custom-call | tf_op jit(solution)/shard_map/copy_out/pallas_call | solution.py:531

commit v4 on v3

--- a/solution.py
+++ b/solution.py
@@ -236,16 +236,6 @@
         enter_whole(0)
         enter_whole(3)
 
-    enter_split(1)
-    enter_split(2)
-
-    @pl.when(half == second)
-    def _():
-        enter_whole(0)
-        enter_whole(3)
-
-    enter_split(0)
-    enter_split(3)
 
     make_tables(
         half * TILES_DEV, (frame - 1) * TILES_DEV, lambda i, e: key_tiles[i, e], lambda i: key_count[i], slot_of, bias_of, entry_of
@@ -291,7 +281,7 @@
     for task in range(2):
         take_near(task + 1 - core, task)
 
-    def queries(task, table, first_tile, at):
+    def queries(task, table, first_tile, at, between=None):
         def score_of(i, scores):
             def one(e, best):
                 return score(e, table + i, first_tile, slot_of, bias_of, kw, held[0, task, tile_rows(i), :], scores, best)
@@ -315,7 +305,12 @@
         best = no_best()
         for e in range(ENTRIES):
             best = score_of(0, scores_even)(e, best)
-        lax.fori_loop(0, TILES_DEV // 2, two, best)
+        if between is None:
+            lax.fori_loop(0, TILES_DEV // 2, two, best)
+        else:
+            best = two(0, best)
+            between()
+            two(1, best)
 
     def q_of(task, i):
         return held[0, task, i * TILE : (i + 1) * TILE, :]
@@ -352,19 +347,29 @@
 
     wait_in(0, first)
     wait_in(3, first)
+    enter_split(1)
+    enter_split(2)
+
+    @pl.when(half == second)
+    def _():
+        enter_whole(0)
+        enter_whole(3)
+
     queries(first, first * TILES_DEV, 2 * first * TILES_DEV, first * TILES_DEV)
-    leave_whole(0, first)
-    leave_whole(1, first)
-    keys(to_near(2 * first), whole_parts(first, 2 * first))
-    hand_over(2 * first, 0, first, twin)
-    keys(to_own(first), whole_parts(first, 1))
-
     for kv in range(2):
         wait_in(1 + kv, 2)
         for way in range(2):
             send(
                 held.at[1 + kv, 2], near_b.at[1 - way, kv], near_b_send.at[way, kv], near_b_recv.at[1 - way, kv], neighbours[way]
             )
+
+    enter_split(0)
+    enter_split(3)
+    leave_whole(0, first)
+    leave_whole(1, first)
+    keys(to_near(2 * first), whole_parts(first, 2 * first))
+    hand_over(2 * first, 0, first, twin)
+    keys(to_own(first), whole_parts(first, 1))
 
     take_near(2 * core, 2)
     wait_in(0, second)
@@ -391,28 +396,26 @@
             spread(TILES_DEV + j, kv, held[1 + kv, 2, tile_rows(j), :])
             spread(2 * TILES_DEV + j, kv, near_b[1, kv, tile_rows(j), :])
 
-    queries(2, half * TILES_DEV, 0, 0)
-    leave_split(0)
-    leave_split(1)
-
-    for at in range(3):
-        for kv in range(2):
-            wait_bytes(from_a.at[at, kv], from_a_recv.at[at, kv])
-
-    for task in range(2):
-        border = (core == task).astype(F32)
-
-        @pl.loop(0, TILES_DEV)
-        def _(j):
-            rows = tile_rows(j)
-            for kv, own in ((0, dk_own), (1, dv_own)):
-                total = own[task, rows, :] + from_a[task, kv, rows, :].astype(F32)
-                total = total + border * from_a[2, kv, rows, :].astype(F32)
-                leaving[2 + kv, task, rows, :] = total.astype(BF16)
-
-        leave_whole(2, task)
-        leave_whole(3, task)
-
+    def finish_whole():
+        for at in range(3):
+            for kv in range(2):
+                wait_bytes(from_a.at[at, kv], from_a_recv.at[at, kv])
+
+        for task in range(2):
+            border = (core == task).astype(F32)
+
+            @pl.loop(0, TILES_DEV)
+            def _(j):
+                rows = tile_rows(j)
+                for kv, own in ((0, dk_own), (1, dv_own)):
+                    total = own[task, rows, :] + from_a[task, kv, rows, :].astype(F32)
+                    total = total + border * from_a[2, kv, rows, :].astype(F32)
+                    leaving[2 + kv, task, rows, :] = total.astype(BF16)
+
+            leave_whole(2, task)
+            leave_whole(3, task)
+
+    queries(2, half * TILES_DEV, 0, 0, finish_whole)
     for way in (0, 1):
         def put(rows, dk, dv):
             to_b[way, 0, rows, :] = dk.astype(BF16)
@@ -421,6 +424,9 @@
         keys(put, (half * TILES_DEV, 0, 2, 2 * way))
         for kv in range(2):
             send(to_b.at[way, kv], from_b.at[1 - way, kv], to_b_send.at[way, kv], from_b_recv.at[1 - way, kv], neighbours[way])
+    leave_split(0)
+    leave_split(1)
+
     keys(to_own(0), (half * TILES_DEV, 0, 2, 1))
 
     for kv, own in ((0, dk_own), (1, dv_own)):

time: 100 us -> 97.9 us (0.979)
  the two profiles are of different devices: /device:TPU:100 before, /device:TPU:4 now
where the time goes in v4:
time: 97.9 us; the launch traced here: 97.8 us
  Pallas kernels  97 us (99%)
    pallas_call x1, Pallas kernels, on_device(): pl.pallas_call(body, out_shape=shapes, in_specs=[smem, smem] + [hbm] * 4,...  94.1 us
    pallas_call x1, Pallas kernels, on_device(): pl.pallas_call(copy_out, out_shape=shapes, in_specs=[hbm] * 4, out_specs=...  2.86 us

profile of v4, /device:TPU:4, one launch (start us, length us, event | category | flops | bytes accessed | tf_op | source)
XLA Modules:
  0.0 97.8 jit_solution(13730789304893809527)
XLA Ops:
  0.6 94.1 %tile_attention.1 = (bf16[128,3072]{1,0:T(8,128)(2,1)}, bf16[128,3072]{1,0:T(8,128)(2,1)}, bf16[128,3072]{1,0:T(8,128)(2,1)}, bf16[128,3072]{1,0:T(8,128)(2,1)}) custom-call(s32[4,8]{1,0:T(4,128)} %refs_0_.1, s32[4]{0:T(128)} %refs_1_.1, bf16[128,3072]{1,0:T(8,128)(2,1)} %refs_2_.1, bf16[128,3072]{1,0:T(8,128)(2,1)} %refs_3_.1, bf16[128,3072]{1,0:T(8,128)(2,1)} %refs_4_.1, ...), custom_call_target="tpu_custom_call" | custom-call | tf_op jit(solution)/shard_map/tile_attention/pallas_call | solution.py:488
  94.8 2.9 %copy_out.1 = (bf16[128,3072]{1,0:T(8,128)(2,1)}, bf16[128,3072]{1,0:T(8,128)(2,1)}, bf16[128,3072]{1,0:T(8,128)(2,1)}, bf16[128,3072]{1,0:T(8,128)(2,1)}) custom-call(bf16[128,3072]{1,0:T(8,128)(2,1)} %get-tuple-element.8.refs_0_, bf16[128,3072]{1,0:T(8,128)(2,1)} %get-tuple-element.9.refs_1_, bf16[128,3072]{1,0:T(8,128)(2,1)} %get-tuple-element.10.refs_2_, ...), custom_call_target="tpu_custom_call" | custom-call | tf_op jit(solution)/shard_map/copy_out/pallas_call | solution.py:537

commit v5 on v3

--- a/solution.py
+++ b/solution.py
@@ -228,6 +228,14 @@
 
     send(table_to, table_from, table_sems.at[0], table_sems.at[1], table_peer)
     first, second = 1 - core, core
+    for t in (1, 2, 0, 3):
+        enter_split(t)
+    for kv in range(2):
+        wait_in(1 + kv, 2)
+        for way in range(2):
+            send(
+                held.at[1 + kv, 2], near_b.at[1 - way, kv], near_b_send.at[way, kv], near_b_recv.at[1 - way, kv], neighbours[way]
+            )
     enter_whole(1)
     enter_whole(2)
 
@@ -235,17 +243,6 @@
     def _():
         enter_whole(0)
         enter_whole(3)
-
-    enter_split(1)
-    enter_split(2)
-
-    @pl.when(half == second)
-    def _():
-        enter_whole(0)
-        enter_whole(3)
-
-    enter_split(0)
-    enter_split(3)
 
     make_tables(
         half * TILES_DEV, (frame - 1) * TILES_DEV, lambda i, e: key_tiles[i, e], lambda i: key_count[i], slot_of, bias_of, entry_of
@@ -261,23 +258,9 @@
         lambda i, e: far_table[i, e], lambda i: far_table[i, ENTRIES], slot_of, bias_of, entry_of,
     )
 
-    for kv in range(2):
-        for task in range(2):
-            wait_in(1 + kv, task)
-            send(
-                held.at[1 + kv, task], near_a.at[task + core, kv], near_a_send.at[task, kv], near_a_recv.at[task, kv], twin
-            )
-        send(held.at[1 + kv, core], near_a.at[2 - 2 * core, kv], near_a_send.at[2, kv], near_a_recv.at[2, kv], above)
-
     def spread(tile, kv, block):
         (kw, vw)[kv][tile] = block
         (kt, vt)[kv][tile] = block.T
-
-    @pl.loop(0, TILES_DEV)
-    def _(j):
-        for kv in range(2):
-            for task in range(2):
-                spread((2 * task + 1) * TILES_DEV + j, kv, held[1 + kv, task, tile_rows(j), :])
 
     def take_near(slot, sem):
         for kv in range(2):
@@ -287,9 +270,6 @@
         def _(j):
             for kv in range(2):
                 spread(2 * slot * TILES_DEV + j, kv, near_a[slot, kv, tile_rows(j), :])
-
-    for task in range(2):
-        take_near(task + 1 - core, task)
 
     def queries(task, table, first_tile, at):
         def score_of(i, scores):
@@ -350,6 +330,59 @@
         for kv in range(2):
             send(to_a.at[slot, kv], from_a.at[at, kv], to_a_send.at[sem, kv], from_a_recv.at[at, kv], to)
 
+    @pl.loop(0, TILES_DEV)
+    def _(j):
+        for kv in range(2):
+            spread(WIDE + TILES_DEV + j, kv, held[1 + kv, 2, tile_rows(j), :])
+
+    wait_in(0, 2)
+    wait_in(3, 2)
+    for way in range(2):
+        for kv in range(2):
+            wait_bytes(near_b.at[way, kv], near_b_recv.at[way, kv])
+
+    @pl.loop(0, TILES_DEV)
+    def _(j):
+        for kv in range(2):
+            for way in range(2):
+                spread(WIDE + 2 * way * TILES_DEV + j, kv, near_b[way, kv, tile_rows(j), :])
+
+    queries(2, half * TILES_DEV, WIDE, 0)
+
+    for kv in range(2):
+        for task in range(2):
+            wait_in(1 + kv, task)
+            send(
+                held.at[1 + kv, task], near_a.at[task + core, kv], near_a_send.at[task, kv], near_a_recv.at[task, kv], twin
+            )
+        send(held.at[1 + kv, core], near_a.at[2 - 2 * core, kv], near_a_send.at[2, kv], near_a_recv.at[2, kv], above)
+
+    @pl.when(half == second)
+    def _():
+        enter_whole(0)
+        enter_whole(3)
+
+    for way in (0, 1):
+        def put(rows, dk, dv):
+            to_b[way, 0, rows, :] = dk.astype(BF16)
+            to_b[way, 1, rows, :] = dv.astype(BF16)
+
+        keys(put, (half * TILES_DEV, 0, 2, 2 * way))
+        for kv in range(2):
+            send(to_b.at[way, kv], from_b.at[1 - way, kv], to_b_send.at[way, kv], from_b_recv.at[1 - way, kv], neighbours[way])
+    leave_split(0)
+    leave_split(1)
+    keys(to_own(2), (half * TILES_DEV, 0, 2, 1))
+
+    @pl.loop(0, TILES_DEV)
+    def _(j):
+        for kv in range(2):
+            for task in range(2):
+                spread((2 * task + 1) * TILES_DEV + j, kv, held[1 + kv, task, tile_rows(j), :])
+
+    for task in range(2):
+        take_near(task + 1 - core, task)
+
     wait_in(0, first)
     wait_in(3, first)
     queries(first, first * TILES_DEV, 2 * first * TILES_DEV, first * TILES_DEV)
@@ -359,81 +392,46 @@
     hand_over(2 * first, 0, first, twin)
     keys(to_own(first), whole_parts(first, 1))
 
-    for kv in range(2):
-        wait_in(1 + kv, 2)
-        for way in range(2):
-            send(
-                held.at[1 + kv, 2], near_b.at[1 - way, kv], near_b_send.at[way, kv], near_b_recv.at[1 - way, kv], neighbours[way]
-            )
+    for way in range(2):
+        for kv in range(2):
+            wait_bytes(from_b.at[way, kv], from_b_recv.at[way, kv])
+
+    @pl.loop(0, TILES_DEV)
+    def _(j):
+        rows = tile_rows(j)
+        for kv, own in ((0, dk_own), (1, dv_own)):
+            total = own[2, rows, :] + from_b[0, kv, rows, :].astype(F32) + from_b[1, kv, rows, :].astype(F32)
+            leaving[2 + kv, 2, rows, :] = total.astype(BF16)
+
+    leave_split(2)
+    leave_split(3)
 
     take_near(2 * core, 2)
     wait_in(0, second)
     wait_in(3, second)
     queries(second, second * TILES_DEV, 2 * second * TILES_DEV, second * TILES_DEV)
+    keys(to_near(2 * second), whole_parts(second, 2 * second))
+    hand_over(2 * second, 1, 2, above)
     leave_whole(0, second)
     leave_whole(1, second)
-    keys(to_near(2 * second), whole_parts(second, 2 * second))
-    hand_over(2 * second, 1, 2, above)
     keys(to_near(1), whole_parts(0, 2), whole_parts(1, 0))
     hand_over(1, 2, second, twin)
     keys(to_own(second), whole_parts(second, 1))
 
-    wait_in(0, 2)
-    wait_in(3, 2)
-    for way in range(2):
-        for kv in range(2):
-            wait_bytes(near_b.at[way, kv], near_b_recv.at[way, kv])
-
-    @pl.loop(0, TILES_DEV)
-    def _(j):
-        for kv in range(2):
-            spread(j, kv, near_b[0, kv, tile_rows(j), :])
-            spread(TILES_DEV + j, kv, held[1 + kv, 2, tile_rows(j), :])
-            spread(2 * TILES_DEV + j, kv, near_b[1, kv, tile_rows(j), :])
-
-    queries(2, half * TILES_DEV, 0, 0)
-    leave_split(0)
-    leave_split(1)
-
-    for at in range(3):
-        for kv in range(2):
-            wait_bytes(from_a.at[at, kv], from_a_recv.at[at, kv])
-
-    for task in range(2):
-        border = (core == task).astype(F32)
-
-        @pl.loop(0, TILES_DEV)
-        def _(j):
-            rows = tile_rows(j)
-            for kv, own in ((0, dk_own), (1, dv_own)):
-                total = own[task, rows, :] + from_a[task, kv, rows, :].astype(F32)
-                total = total + border * from_a[2, kv, rows, :].astype(F32)
+    for task, others in ((first, (first,)), (second, (second, 2))):
+        for kv, own in ((0, dk_own), (1, dv_own)):
+            for at in others:
+                wait_bytes(from_a.at[at, kv], from_a_recv.at[at, kv])
+
+            @pl.loop(0, TILES_DEV)
+            def _(j):
+                rows = tile_rows(j)
+                total = own[task, rows, :]
+                for at in others:
+                    total = total + from_a[at, kv, rows, :].astype(F32)
                 leaving[2 + kv, task, rows, :] = total.astype(BF16)
 
-        leave_whole(2, task)
-        leave_whole(3, task)
-
-    for way in (0, 1):
-        def put(rows, dk, dv):
-            to_b[way, 0, rows, :] = dk.astype(BF16)
-            to_b[way, 1, rows, :] = dv.astype(BF16)
-
-        keys(put, (half * TILES_DEV, 0, 2, 2 * way))
-        for kv in range(2):
-            send(to_b.at[way, kv], from_b.at[1 - way, kv], to_b_send.at[way, kv], from_b_recv.at[1 - way, kv], neighbours[way])
-    keys(to_own(0), (half * TILES_DEV, 0, 2, 1))
-
-    for kv, own in ((0, dk_own), (1, dv_own)):
-        for way in range(2):
-            wait_bytes(from_b.at[way, kv], from_b_recv.at[way, kv])
-
-        @pl.loop(0, TILES_DEV)
-        def _(j):
-            rows = tile_rows(j)
-            total = own[0, rows, :] + from_b[0, kv, rows, :].astype(F32) + from_b[1, kv, rows, :].astype(F32)
-            leaving[2 + kv, 2, rows, :] = total.astype(BF16)
-
-        leave_split(2 + kv)
+            leave_whole(2 + kv, task)
 
     seven = SLAB - 128
     for t in range(4):
@@ -499,17 +497,17 @@
             pltpu.VMEM((2, 2) + block, BF16),
             pltpu.VMEM((2, 2) + block, BF16),
             pltpu.VMEM((4, 3) + block, BF16),
-            pltpu.VMEM((WIDE, TILE, HEAD_DIM), BF16),
-            pltpu.VMEM((WIDE, TILE, HEAD_DIM), BF16),
-            pltpu.VMEM((WIDE, HEAD_DIM, TILE), BF16),
-            pltpu.VMEM((WIDE, HEAD_DIM, TILE), BF16),
+            pltpu.VMEM((WIDE + NEAR, TILE, HEAD_DIM), BF16),
+            pltpu.VMEM((WIDE + NEAR, TILE, HEAD_DIM), BF16),
+            pltpu.VMEM((WIDE + NEAR, HEAD_DIM, TILE), BF16),
+            pltpu.VMEM((WIDE + NEAR, HEAD_DIM, TILE), BF16),
             pltpu.VMEM((ENTRIES, TILE, TILE), F32),
             pltpu.VMEM((ENTRIES, TILE, TILE), F32),
             pltpu.VMEM((2 * TILES_DEV, ENTRIES + 1, TILE, TILE), BF16),
             pltpu.VMEM((2 * TILES_DEV, ENTRIES + 1, TILE, TILE), BF16),
             pltpu.VMEM((2 * TILES_DEV, HEAD_DIM, TILE), BF16),
-            pltpu.VMEM((2,) + block, F32),
-            pltpu.VMEM((2,) + block, F32),
+            pltpu.VMEM((3,) + block, F32),
+            pltpu.VMEM((3,) + block, F32),
             dma((4, 3)),
             dma((4, 3)),
             dma((3, 2)),

time: 100 us -> 101 us (1.010)
  the two profiles are of different devices: /device:TPU:100 before, /device:TPU:128 now
where the time goes in v5:
time: 101 us
  Pallas kernels  101 us (100%)
    pallas_call x1, Pallas kernels, on_device(): pl.pallas_call(body, out_shape=shapes, in_specs=[smem, smem] + [hbm] * 4,...  97.7 us
    pallas_call x1, Pallas kernels, on_device(): pl.pallas_call(copy_out, out_shape=shapes, in_specs=[hbm] * 4, out_specs=...  2.86 us

profile of v5, /device:TPU:128, one launch (start us, length us, event | category | flops | bytes accessed | tf_op | source)
XLA Modules:
  0.0 101.4 jit_solution(10395600023636711600)
XLA Ops:
  0.6 97.7 %tile_attention.1 = (bf16[128,3072]{1,0:T(8,128)(2,1)}, bf16[128,3072]{1,0:T(8,128)(2,1)}, bf16[128,3072]{1,0:T(8,128)(2,1)}, bf16[128,3072]{1,0:T(8,128)(2,1)}) custom-call(s32[4,8]{1,0:T(4,128)} %refs_0_.1, s32[4]{0:T(128)} %refs_1_.1, bf16[128,3072]{1,0:T(8,128)(2,1)} %refs_2_.1, bf16[128,3072]{1,0:T(8,128)(2,1)} %refs_3_.1, bf16[128,3072]{1,0:T(8,128)(2,1)} %refs_4_.1, ...), custom_call_target="tpu_custom_call" | custom-call | tf_op jit(solution)/shard_map/tile_attention/pallas_call | solution.py:480
  98.3 2.9 %copy_out.1 = (bf16[128,3072]{1,0:T(8,128)(2,1)}, bf16[128,3072]{1,0:T(8,128)(2,1)}, bf16[128,3072]{1,0:T(8,128)(2,1)}, bf16[128,3072]{1,0:T(8,128)(2,1)}) custom-call(bf16[128,3072]{1,0:T(8,128)(2,1)} %get-tuple-element.8.refs_0_, bf16[128,3072]{1,0:T(8,128)(2,1)} %get-tuple-element.9.refs_1_, bf16[128,3072]{1,0:T(8,128)(2,1)} %get-tuple-element.10.refs_2_, ...), custom_call_target="tpu_custom_call" | custom-call | tf_op jit(solution)/shard_map/copy_out/pallas_call | solution.py:529

commit v6 on v4

--- a/solution.py
+++ b/solution.py
@@ -236,6 +236,14 @@
         enter_whole(0)
         enter_whole(3)
 
+    enter_split(1)
+    enter_split(2)
+
+    @pl.when(half == second)
+    def _():
+        enter_whole(0)
+        enter_whole(3)
+
 
     make_tables(
         half * TILES_DEV, (frame - 1) * TILES_DEV, lambda i, e: key_tiles[i, e], lambda i: key_count[i], slot_of, bias_of, entry_of
@@ -347,14 +355,6 @@
 
     wait_in(0, first)
     wait_in(3, first)
-    enter_split(1)
-    enter_split(2)
-
-    @pl.when(half == second)
-    def _():
-        enter_whole(0)
-        enter_whole(3)
-
     queries(first, first * TILES_DEV, 2 * first * TILES_DEV, first * TILES_DEV)
     for kv in range(2):
         wait_in(1 + kv, 2)

time: 97.9 us -> 97.2 us (level)
  the two profiles are of different devices: /device:TPU:4 before, /device:TPU:100 now
where the time goes in v6:
time: 97.2 us; the launch traced here: 95.5 us
  Pallas kernels  94.7 us (97%)
    pallas_call x1, Pallas kernels, on_device(): pl.pallas_call(body, out_shape=shapes, in_specs=[smem, smem] + [hbm] * 4,...  91.9 us
    pallas_call x1, Pallas kernels, on_device(): pl.pallas_call(copy_out, out_shape=shapes, in_specs=[hbm] * 4, out_specs=...  2.86 us

profile of v6, /device:TPU:100, one launch (start us, length us, event | category | flops | bytes accessed | tf_op | source)
XLA Modules:
  0.0 95.5 jit_solution(12425485111429079216)
XLA Ops:
  0.6 91.9 %tile_attention.1 = (bf16[128,3072]{1,0:T(8,128)(2,1)}, bf16[128,3072]{1,0:T(8,128)(2,1)}, bf16[128,3072]{1,0:T(8,128)(2,1)}, bf16[128,3072]{1,0:T(8,128)(2,1)}) custom-call(s32[4,8]{1,0:T(4,128)} %refs_0_.1, s32[4]{0:T(128)} %refs_1_.1, bf16[128,3072]{1,0:T(8,128)(2,1)} %refs_2_.1, bf16[128,3072]{1,0:T(8,128)(2,1)} %refs_3_.1, bf16[128,3072]{1,0:T(8,128)(2,1)} %refs_4_.1, ...), custom_call_target="tpu_custom_call" | custom-call | tf_op jit(solution)/shard_map/tile_attention/pallas_call | solution.py:488
  92.5 2.9 %copy_out.1 = (bf16[128,3072]{1,0:T(8,128)(2,1)}, bf16[128,3072]{1,0:T(8,128)(2,1)}, bf16[128,3072]{1,0:T(8,128)(2,1)}, bf16[128,3072]{1,0:T(8,128)(2,1)}) custom-call(bf16[128,3072]{1,0:T(8,128)(2,1)} %get-tuple-element.8.refs_0_, bf16[128,3072]{1,0:T(8,128)(2,1)} %get-tuple-element.9.refs_1_, bf16[128,3072]{1,0:T(8,128)(2,1)} %get-tuple-element.10.refs_2_, ...), custom_call_target="tpu_custom_call" | custom-call | tf_op jit(solution)/shard_map/copy_out/pallas_call | solution.py:537
